TPU v7x, 32 devices: a whole 2x2x4 slice. The times are simulated.
32 devices in a mesh: grp: 4 (over x, core), blk: 8 (over z, y).
Axes of the slice: x: 2, y: 2, z: 4, core: 2. Of those that a mesh axis runs over, the one named last changes fastest.
Arguments:
- pair_density: bfloat16 [2048, 8192], P('grp', 'blk'), may hold values from -14 to 14
- energies: float32 [2048], P('grp'), may hold values from 1 to 4
- batch_live: int32 [4], replicated, may hold values from 1 to 512, 1280 in all
- coulomb_root: float32 [8192], replicated, may hold values from 0.5 to 2
Outputs:
- polarized: bfloat16 [4, 8192, 8192], P('grp', 'blk')
- screened: float32 [4, 8192, 128], P('grp', 'blk')
Inputs may be any that keep to these rules, and one draw needn't show every extreme that they name: Group g's live transitions are its first batch_live[g] slots of 512; at least one group is full.
All inputs are finite; a program needn't handle non-finite values.
Results may differ from a plain program's by a relative error of at most 0.03.
Values may be sent and summed in bfloat16 or wider, within the bound.
A program may use at most 128 MiB of HBM per device.

v0:
```python
import functools
import math

import jax
import jax.numpy as jnp
from jax import lax
from jax.experimental import pallas as pl
from jax.experimental.pallas import tpu as pltpu
from jax.sharding import PartitionSpec as P

G = 8192
CW = 128
DYSON = 2
LANES = 128


def live_weights(all_energy, batch_live, slots, total_slots, group_ids, frequencies, norm_factor):
    positions = jnp.arange(total_slots, dtype=jnp.int32)
    owner_match = (positions // slots)[:, None] == group_ids[None, :]
    limits = jnp.sum(jnp.where(owner_match, batch_live[None, :], 0), axis=1)
    is_live = (positions % slots < limits).astype(jnp.float32)
    weight = (
        -2.0
        * all_energy[None, :]
        / (all_energy[None, :] * all_energy[None, :] + frequencies[:, None] * frequencies[:, None])
    )
    return weight * is_live[None, :] * norm_factor


def plain_body(pair_density, energies, batch_live, coulomb_root):
    slots = pair_density.shape[0]
    width_own = pair_density.shape[1]
    group_count = lax.axis_size("grp")
    block_count = lax.axis_size("blk")
    total_slots = slots * group_count
    group_index = lax.axis_index("grp")
    block_index = lax.axis_index("blk")
    norm_factor = 1.0 / math.sqrt(total_slots)
    own_root = lax.dynamic_slice_in_dim(coulomb_root, block_index * width_own, width_own)
    group_ids = jnp.arange(group_count, dtype=jnp.int32)
    row_density, all_energy = (
        lax.all_gather(pair_density, "grp", axis=0, tiled=True),
        lax.all_gather(energies.astype(jnp.bfloat16), "grp", axis=0, tiled=True).astype(
            energies.dtype
        ),
    )
    frequencies = 0.6 * jnp.arange(group_count, dtype=jnp.float32)
    weight = live_weights(
        all_energy, batch_live, slots, total_slots, group_ids, frequencies, norm_factor
    )
    scaled = (weight[:, :, None] * row_density.astype(jnp.float32)[None, :, :]).astype(jnp.bfloat16)
    sub_width = width_own // group_count
    my_slice = lax.dynamic_slice_in_dim(row_density, group_index * sub_width, sub_width, 1)
    root_table = jnp.reshape(coulomb_root, (block_count, group_count, sub_width))
    my_roots = jnp.reshape(
        lax.dynamic_index_in_dim(root_table, group_index, 1, keepdims=False), (-1,)
    )
    chi = jnp.einsum(
        "ftc,tk->fck",
        scaled,
        lax.all_gather(my_slice, "blk", axis=1, tiled=True),
        preferred_element_type=jnp.float32,
    )
    quarter = own_root[None, :, None] * chi * my_roots[None, None, :]
    received = lax.all_to_all(
        quarter.astype(jnp.bfloat16), "grp", split_axis=0, concat_axis=0, tiled=True
    )
    received = jnp.reshape(received, (group_count, width_own, block_count, sub_width))
    polarized = jnp.reshape(
        jnp.transpose(received, (1, 2, 0, 3)), (width_own, width_own * block_count)
    )
    lead_blocks = (CW + width_own - 1) // width_own
    lead = quarter[:, :, : lead_blocks * sub_width]
    lead_back = lax.all_to_all(
        lead.astype(jnp.bfloat16), "grp", split_axis=0, concat_axis=0, tiled=True
    ).astype(lead.dtype)
    lead_back = jnp.reshape(lead_back, (group_count, width_own, lead_blocks, sub_width))
    window = jnp.reshape(
        jnp.transpose(lead_back, (1, 2, 0, 3)), (width_own, lead_blocks * width_own)
    )[:, :CW]
    state = window
    for dyson_step in range(DYSON):
        rounded = state.astype(jnp.bfloat16)
        product = jnp.dot(
            polarized,
            lax.all_gather(rounded, "blk", axis=0, tiled=True),
            preferred_element_type=jnp.float32,
        )
        state = window + 8.0 / G * product
    return (polarized[None], state[None])


def pack_rows(batch_live, slots, total, packed):
    ends = jnp.cumsum(batch_live)
    starts = ends - batch_live
    j = jnp.arange(packed, dtype=jnp.int32)
    in_group = (j[:, None] >= starts[None, :]) & (j[:, None] < ends[None, :])
    group_base = jnp.arange(batch_live.shape[0], dtype=jnp.int32) * slots - starts
    source = jnp.sum(jnp.where(in_group, group_base[None, :] + j[:, None], 0), axis=1)
    used = jnp.any(in_group, axis=1)
    source = jnp.where(used, source, -1)
    return source, used


def chi_kernel(
    n, factor, own_ref, p_ref, w_ref, own_root_ref, r_ref, out_ref, s_ref,
    at_ref, q_ref, u_ref, v_ref, t_ref,
):
    i = pl.program_id(0)
    width = at_ref.shape[0] - CW
    split, _, _, sub = p_ref.shape

    def root(k):
        return r_ref[:, k * sub:(k + 1) * sub]

    def spread(k, part):
        part = (part * root(k)).T.astype(jnp.bfloat16)
        return jnp.dot(p_ref[k, 0], part, preferred_element_type=jnp.float32)

    @pl.when(i == 0)
    def _():
        for k in range(split):
            part = slice(k * sub, (k + 1) * sub)
            left = (own_ref[k].astype(jnp.float32) * own_root_ref[:, part]).T
            at_ref[part] = (left * w_ref[...]).astype(jnp.bfloat16)
        q = (p_ref[0, 0, :, :CW].astype(jnp.float32) * r_ref[:, :CW]).T
        q_ref[...] = q
        at_ref[width:] = (q * w_ref[...]).astype(jnp.bfloat16)
        u_ref[...] = jnp.zeros_like(u_ref)

    @pl.when(i < n)
    def _():
        for k in range(split):
            prod = jnp.dot(at_ref[...], p_ref[k, 0], preferred_element_type=jnp.float32) * root(k)
            out_ref[:, k * sub:(k + 1) * sub] = prod[:width].astype(jnp.bfloat16)
            t_ref[:, k * sub:(k + 1) * sub] = prod[width:]

    @pl.when(i < n)
    def _():
        for k in range(split):
            u_ref[...] += spread(k, t_ref[:, k * sub:(k + 1) * sub])

    @pl.when(i == n - 1)
    def _():
        v_ref[...] = (u_ref[...].T * (w_ref[...] * factor)).astype(jnp.bfloat16)

    @pl.when(i >= n)
    def _():
        for k in range(split):
            prod = jnp.dot(v_ref[...], p_ref[k, 0], preferred_element_type=jnp.float32) * root(k)
            u_ref[...] += spread(k, prod)

    @pl.when(i == 2 * n - 1)
    def _():
        x = (q_ref[...] + factor * u_ref[...].T).astype(jnp.bfloat16)
        s_ref[...] = lax.dot_general(
            at_ref[:width], x, (((1,), (1,)), ((), ())), preferred_element_type=jnp.float32)


def chi_and_screen(own, pieces, weight, own_root, coulomb_root):
    split, n, packed, sub = pieces.shape
    width = split * sub
    return pl.pallas_call(
        functools.partial(chi_kernel, n, 8.0 / G),
        grid=(2 * n,),
        out_shape=(
            jax.ShapeDtypeStruct((width, n * split * sub), jnp.bfloat16),
            jax.ShapeDtypeStruct((width, CW), jnp.float32),
        ),
        in_specs=[
            pl.BlockSpec((split, packed, sub), lambda i: (0, 0, 0)),
            pl.BlockSpec((split, 1, packed, sub), lambda i: (0, i % n, 0, 0)),
            pl.BlockSpec((1, packed), lambda i: (0, 0)),
            pl.BlockSpec((1, width), lambda i: (0, 0)),
            pl.BlockSpec((1, split * sub), lambda i: (0, i % n)),
        ],
        out_specs=(
            pl.BlockSpec((width, split * sub), lambda i: (0, jnp.minimum(i, n - 1))),
            pl.BlockSpec((width, CW), lambda i: (0, 0)),
        ),
        scratch_shapes=[
            pltpu.VMEM((width + CW, packed), jnp.bfloat16),
            pltpu.VMEM((CW, packed), jnp.float32),
            pltpu.VMEM((packed, CW), jnp.float32),
            pltpu.VMEM((CW, packed), jnp.bfloat16),
            pltpu.VMEM((CW, width), jnp.float32),
        ],
        compiler_params=pltpu.CompilerParams(vmem_limit_bytes=48 * 1024 * 1024),
    )(own, pieces, weight[None, :], own_root[None, :], coulomb_root[None, :])


def gather_kernel(
    nz, rows_ref, energy_ref, source_ref, out_ref, energies_ref, own_ref,
    all_ref, pick_ref, recv, s_up, s_down, s_y, s_x, s_pair, s_own,
    r_rows, s_rows, s_local, r_energy, s_energy,
):
    g, b = lax.axis_index("grp"), lax.axis_index("blk")
    x, c = g // 2, g % 2
    z, y = b // 2, b % 2
    half = own_ref.shape[1] // 2
    rows = pl.ds(pl.multiple_of(c * half, half), half)
    other_rows = pl.ds(pl.multiple_of((1 - c) * half, half), half)
    to_up, to_down = (g, b + 2), (g, b - 2)
    to_y = (g, z * 2 + 1 - y)
    to_x = ((1 - x) * 2 + c, b)
    to_pair = (x * 2 + 1 - c, b)
    has_up, has_down = z + 1 < nz, z >= 1
    skip_y, own_x = 2 * (1 - x), 2 * x

    def copy(q, bb, sem, to, own=False):
        src = own_ref.at[q, rows] if own else out_ref.at[q, bb, rows]
        return pltpu.make_async_remote_copy(
            src_ref=src, dst_ref=out_ref.at[q, bb, rows], send_sem=sem,
            recv_sem=recv.at[q, bb, c], device_id=to, device_id_type=pl.DeviceIdType.MESH)

    def arrived(q, bb):
        copy(q, bb, s_pair.at[q, bb], to_pair).wait_recv()

    def up(zz, j, own=False):
        return copy(x + j, zz * 2 + y, s_up.at[j, zz], to_up, own)

    def down(zz, j, own=False):
        return copy(x + j, zz * 2 + y, s_down.at[j, zz], to_down, own)

    def over_y(zz, j, own=False):
        return copy(x + j, zz * 2 + y, s_y.at[j, zz], to_y, own)

    def over_x(zz, yy, j):
        return copy(x + j, zz * 2 + yy, s_x.at[j, zz * 2 + yy], to_x)

    def over_pair(q, bb):
        return copy(q, bb, s_pair.at[q, bb], to_pair)

    def takes_y(zz, j):
        return (zz % 4 != 1) | (j != skip_y)

    def other_y_takes_x(zz, j):
        return ((zz % 4 != 1) & (j == own_x)) | ((zz % 4 == 1) & (j != skip_y))

    def when(condition, make, act):
        @pl.when(condition)
        def _():
            getattr(make(), act)()

    def from_z(zz, j, below, valid):
        @pl.when(valid)
        def _():
            q, bb = x + j, zz * 2 + y
            arrived(q, bb)
            if below:
                when(has_up, lambda: up(zz, j), "start")
            else:
                when(has_down, lambda: down(zz, j), "start")
            when(takes_y(zz, j), lambda: over_y(zz, j), "start")
            when(j == own_x, lambda: over_x(zz, y, j), "start")
            over_pair(q, bb).start()

    def from_y(zz, j, valid):
        @pl.when(valid & takes_y(zz, j))
        def _():
            q, bb = x + j, zz * 2 + 1 - y
            arrived(q, bb)
            when(other_y_takes_x(zz, j), lambda: over_x(zz, 1 - y, j), "start")
            over_pair(q, bb).start()

    def from_x(zz, same_y, valid):
        bb = zz * 2 + (y if same_y else 1 - y)

        def take(q):
            arrived(q, bb)
            over_pair(q, bb).start()

        if same_y:
            @pl.when(valid)
            def _():
                take(3 * (1 - x))
        else:
            @pl.when(valid & (zz % 4 != 1))
            def _():
                take(3 * (1 - x))

            @pl.when(valid & (zz % 4 == 1))
            def _():
                take(2 * (1 - x))
                take(2 * (1 - x) + 1)

    def at_distance(d):
        if d == 0:
            return [(z, True, z >= 0)]
        return [(z - d, True, z >= d), (z + d, False, z + d < nz)]

    barrier = pltpu.get_barrier_semaphore()

    def greet(to):
        pl.semaphore_signal(barrier, inc=1, device_id=to, device_id_type=pl.DeviceIdType.MESH)

    for to in (to_y, to_x, to_pair):
        greet(to)
    pl.when(has_up)(lambda: greet(to_up))
    pl.when(has_down)(lambda: greet(to_down))
    peers = 3 + has_up.astype(jnp.int32) + has_down.astype(jnp.int32)
    pl.semaphore_wait(barrier, peers)

    slots, packed, sub = rows_ref.shape[0], own_ref.shape[1], own_ref.shape[2]
    g_x, g_pair = (1 - x) * 2 + c, x * 2 + 1 - c
    g_far = (1 - x) * 2 + 1 - c

    def span(k):
        return pl.ds(pl.multiple_of(k * slots, slots), slots)

    def order(j):
        return jnp.where(j < 3, x + j, 3 * (1 - x))

    def rows_to(q, way, to, who):
        dst = all_ref.at[q, span(who)]
        columns = pl.ds(pl.multiple_of(q * sub, sub), sub)
        return pltpu.make_async_remote_copy(
            src_ref=dst if way == 2 else rows_ref.at[:, columns], dst_ref=dst,
            send_sem=s_rows.at[way, q], recv_sem=r_rows.at[q, who], device_id=to,
            device_id_type=pl.DeviceIdType.MESH)

    def rows_local(q):
        columns = pl.ds(pl.multiple_of(q * sub, sub), sub)
        return pltpu.make_async_copy(rows_ref.at[:, columns], all_ref.at[q, span(g)], s_local.at[q])

    def energy_to(way, to, who):
        return pltpu.make_async_remote_copy(
            src_ref=energies_ref.at[who] if way == 2 else energy_ref.at[0],
            dst_ref=energies_ref.at[who], send_sem=s_energy.at[way], recv_sem=r_energy.at[who],
            device_id=to, device_id_type=pl.DeviceIdType.MESH)

    for j in range(4):
        q = order(j)
        rows_to(q, 0, to_x, g).start()
        rows_to(q, 1, to_pair, g).start()
        rows_local(q).start()
    energy_to(0, to_x, g).start()
    energy_to(1, to_pair, g).start()
    keep_energy = pltpu.make_async_copy(energy_ref.at[0], energies_ref.at[g], s_local.at[4])
    keep_energy.start()

    @pl.loop(0, packed // 128)
    def _(k):
        part = pl.ds(pl.multiple_of(k * 128, 128), 128)
        at = lax.broadcasted_iota(jnp.int32, (128, pick_ref.shape[1]), 1)
        pick_ref[part] = (source_ref[part] == at).astype(jnp.float32).astype(jnp.bfloat16)

    def keep(q):
        return pltpu.make_async_copy(own_ref.at[q], out_ref.at[q, b], s_own.at[q])

    @pl.loop(0, 4)
    def _(j):
        q = order(j)
        rows_to(q, 0, to_x, g_x).wait_recv()
        rows_to(q, 2, to_pair, g_x).start()
        rows_local(q).wait()
        rows_to(q, 1, to_pair, g_pair).wait_recv()
        rows_to(q, 2, to_pair, g_far).wait_recv()
        own_ref[q] = jnp.dot(
            pick_ref[...], all_ref[q], preferred_element_type=jnp.float32).astype(jnp.bfloat16)
        carried = j < 3
        when(carried & has_up, lambda: up(z, j, True), "start")
        when(carried & has_down, lambda: down(z, j, True), "start")
        when(carried & takes_y(z, j), lambda: over_y(z, j, True), "start")
        keep(q).start()

    energy_to(0, to_x, g_x).wait_recv()
    energy_to(2, to_pair, g_x).start()

    for s in range(nz + 1):
        for j in range(3):
            if 1 <= s + 1 < nz:
                for zz, below, valid in at_distance(s + 1):
                    from_z(zz, j, below, valid)
            if s < nz:
                for zz, _, valid in at_distance(s):
                    from_y(zz, j, valid)
        if 1 <= s < nz:
            for zz, _, valid in at_distance(s):
                from_x(zz, True, valid)
        if s >= 1:
            for zz, _, valid in at_distance(s - 1):
                from_x(zz, False, valid)

    def from_pair(q, bb):
        pltpu.make_async_remote_copy(
            src_ref=out_ref.at[q, bb, other_rows], dst_ref=out_ref.at[q, bb, other_rows],
            send_sem=s_pair.at[q, bb], recv_sem=recv.at[q, bb, 1 - c],
            device_id=to_pair, device_id_type=pl.DeviceIdType.MESH).wait_recv()
        over_pair(q, bb).wait_send()

    energy_to(1, to_pair, g_pair).wait_recv()
    energy_to(2, to_pair, g_far).wait_recv()
    energy_to(0, to_x, g).wait_send()
    energy_to(1, to_pair, g).wait_send()
    energy_to(2, to_pair, g_x).wait_send()
    keep_energy.wait()
    for j in range(4):
        q = order(j)
        rows_to(q, 0, to_x, g).wait_send()
        rows_to(q, 1, to_pair, g).wait_send()
        rows_to(q, 2, to_pair, g_x).wait_send()
        keep(q).wait()
    for j in range(3):
        when(has_up, lambda: up(z, j, True), "wait_send")
        when(has_down, lambda: down(z, j, True), "wait_send")
        when(takes_y(z, j), lambda: over_y(z, j, True), "wait_send")
    for d in range(nz):
        for zz, below, valid in at_distance(d):
            for j in range(3):
                if d >= 1:
                    if below:
                        when(valid & has_up, lambda: up(zz, j), "wait_send")
                    else:
                        when(valid & has_down, lambda: down(zz, j), "wait_send")
                    when(valid & takes_y(zz, j), lambda: over_y(zz, j), "wait_send")
                    when(valid & (j == own_x), lambda: over_x(zz, y, j), "wait_send")
                when(valid & other_y_takes_x(zz, j), lambda: over_x(zz, 1 - y, j), "wait_send")
            for same_y in (True, False):
                if d >= 1 or not same_y:
                    for q in range(4):
                        pl.when(valid)(
                            lambda q=q: from_pair(q, zz * 2 + (y if same_y else 1 - y)))


def gather_pieces(pair_density, energies, source, blocks, split):
    slots, width = pair_density.shape
    packed = source.shape[0]
    sub, nz = width // split, blocks // 2
    dma = pltpu.SemaphoreType.DMA
    vmem = pl.BlockSpec(memory_space=pltpu.VMEM)
    return pl.pallas_call(
        functools.partial(gather_kernel, nz),
        out_shape=(
            jax.ShapeDtypeStruct((split, blocks, packed, sub), jnp.bfloat16),
            jax.ShapeDtypeStruct((split, 1, slots), jnp.float32),
            jax.ShapeDtypeStruct((split, packed, sub), jnp.bfloat16),
        ),
        in_specs=[vmem, vmem, vmem],
        out_specs=(pl.BlockSpec(memory_space=pl.ANY), vmem, vmem),
        scratch_shapes=[
            pltpu.VMEM((split, split * slots, sub), jnp.bfloat16),
            pltpu.VMEM((packed, split * slots), jnp.bfloat16),
            dma((split, blocks, 2)), dma((3, nz)), dma((3, nz)), dma((3, nz)),
            dma((3, blocks)), dma((split, blocks)), dma((split,)),
            dma((split, split)), dma((3, split)), dma((split + 1,)), dma((split,)), dma((3,)),
        ],
        compiler_params=pltpu.CompilerParams(
            collective_id=0, has_side_effects=True, vmem_limit_bytes=40 * 1024 * 1024),
    )(pair_density, energies[None, None, :], source[:, None])


def body(pair_density, energies, batch_live, coulomb_root):
    slots, width = pair_density.shape
    group_count = lax.axis_size("grp")
    blocks = lax.axis_size("blk")
    total = slots * group_count
    packed = total * 5 // 8
    group_index = lax.axis_index("grp")
    block_index = lax.axis_index("blk")
    own_root = lax.dynamic_slice_in_dim(coulomb_root, block_index * width, width)

    source, used = pack_rows(batch_live, slots, total, packed)
    pieces, all_energy, own = gather_pieces(pair_density, energies, source, blocks, group_count)
    pick = source[:, None] == jnp.arange(total, dtype=jnp.int32)[None, :]
    energy = jnp.sum(jnp.where(pick, jnp.reshape(all_energy, (1, total)), 0.0), axis=1)
    energy = jnp.where(used, energy, 1.0)
    frequency = 0.6 * group_index.astype(jnp.float32)
    weight = -2.0 * energy / (energy * energy + frequency * frequency)
    weight = jnp.where(used, weight, 0.0) * (1.0 / math.sqrt(total))
    polarized, screened = chi_and_screen(own, pieces, weight, own_root, coulomb_root)
    return (polarized[None], screened[None])


def solution(mesh):
    placed = (P("grp", "blk"), P("grp"), P(), P())
    aligned = (
        mesh.shape["grp"] == 4
        and mesh.shape["blk"] % 2 == 0
        and (G // mesh.shape["blk"]) % (LANES * mesh.shape["grp"]) == 0
    )
    return jax.shard_map(
        body if aligned else plain_body,
        mesh=mesh,
        in_specs=placed,
        out_specs=(P("grp", "blk", None), P("grp", "blk", None)),
        check_vma=False,
    )
```

profile of v0, /device:TPU:0, one launch (start us, length us, event | category | flops | bytes accessed | tf_op | source)
XLA Modules:
  0.0 179.2 jit_solution(2429892974477312134)
XLA Ops:
  0.6 0.8 reduce-window.8
  1.5 0.7 multiply_subtract_fusion
  2.1 0.1 fusion.2
  2.2 0.7 dynamic_slice.3
  2.9 0.1 select_reduce_fusion.1
  3.0 0.2 select_n.54.source_ref
  3.3 0.0 copy-start
  3.3 1.2 copy-done
  4.5 0.0 copy-start.2
  4.5 0.7 copy-done.2
  5.2 113.9 %shard_map.59 = (bf16[4,8,1280,256]{3,2,1,0:T(8,128)(2,1)}, f32[4,1,512]{2,1,0:T(1,128)S(1)}, bf16[4,1280,256]{2,1,0:T(8,128)(2,1)S(1)}) custom-call(bf16[512,1024]{1,0:T(8,128)(2,1)S(1)} %copy-done, f32[1,1,512]{2,1,0:T(1,128)S(1)} %bitcast.12, s32[1280,1]{1,0:T(8,128)S(1)} %select_n.54.source_ref), custom_call_target="tpu_custom_call" | custom-call | tf_op jit(solution)/shard_map/pallas_call | solution.py:432
  119.0 1.5 select_reduce_fusion
  120.5 0.0 copy-start.1
  120.5 0.7 copy-done.1
  121.3 57.9 %shard_map.60 = (bf16[1024,8192]{1,0:T(8,128)(2,1)}, f32[1024,128]{1,0:T(8,128)}) custom-call(bf16[4,1280,256]{2,1,0:T(8,128)(2,1)S(1)} %get-tuple-element.7.own_ref, bf16[4,8,1280,256]{3,2,1,0:T(8,128)(2,1)} %get-tuple-element.8.p_ref, f32[1,1280]{1,0:T(1,128)S(1)} %fusion.1.w_ref, f32[1,1024]{1,0:T(1,128)S(1)} %bitcast.11, f32[1,8192]{1,0:T(1,128)S(1)} %bitcast.10), custom_call_target="tpu_custom_call" | custom-call | tf_op jit(solution)/shard_map/pallas_call | solution.py:163
  (2 shorter events, 0.0 us)
Async XLA Ops:
  3.3 1.2 copy-start
  4.5 0.7 copy-start.2
  120.5 0.8 copy-start.1
where the time goes:
time: 181 us; the launch traced here: 179 us
  Pallas kernels  172 us (95%)
  local copies, waits for them, and re-layouts  3.57 us (2%)
  other arithmetic  3.18 us (2%)
    pallas_call x1, Pallas kernels, gather_pieces(): pl.pallas_call(functools.partial(gather_kernel, nz), out_shape=(jax.Shape...  114 us
    pallas_call x1, Pallas kernels, chi_and_screen(): pl.pallas_call(functools.partial(chi_kernel, n, 8.0 / G), grid=(2 * n,),...  57.9 us

commit v1 on v0

v1 whole, which is shorter than its diff:
```python
import functools
import math

import jax
import jax.numpy as jnp
from jax import lax
from jax.experimental import pallas as pl
from jax.experimental.pallas import tpu as pltpu
from jax.sharding import PartitionSpec as P

G = 8192
CW = 128
DYSON = 2
LANES = 128
MESH = pl.DeviceIdType.MESH
VMEM_LIMIT = 34 * 1024 * 1024
FINISH_LIMIT = 30 * 1024 * 1024
OWN, XO, YO, YD, ZN, XN, YN, ZD, RD = range(9)
RELAY_Y = (3,)
EVENTS = (
    0, 1, 2, 3, 16, 17, 18, 19, 32, 33, 34, 35, 48, 49, 50, 51, 68, 69, 70, 71, 72, 73, 74,
    75, 76, 77, 78, 79, 84, 85, 86, 87, 88, 89, 90, 91, 92, 93, 94, 95, 100, 101, 102, 103,
    104, 105, 106, 107, 108, 109, 110, 111, 116, 117, 118, 120, 121, 122, 124, 125, 126, 135,
    139, 143,
)
PLANS = (
    (
        (
            0, 69, 2, 3, 71, 18, 1, 50, 32, 16, 68, 76, 70, 73, 19, 17, 85, 87, 84, 34, 75,
        ),
        (
            1, 0, 5, 2, 4, 12, 3, 8, 13, 9, 11, 7, 15, 10, 14, 6,
        ),
        (
            (108, 92, 48), (), (), (101, 72), (), (33, 35, 105, 78, 86, 74), (89,), (), (49,
            117, 100, 102), (77, 94, 51), (), (116,), (79, 90, 88, 126), (104,), (107, 91), (93,
            103, 95), (), (), (109, 118, 139), (110, 121), (122,), (135,), (), (106, 143, 125,
            111), (120,), (), (), (124,), (), (), (), (),
        ),
        (),
    ),
    (
        (
            1, 0, 2, 17, 3, 70, 68, 74, 73, 75, 16, 76, 84, 72, 86, 49, 18, 34, 32, 78, 100, 19,
            71,
        ),
        (
            0, 4, 1, 6, 8, 12, 5, 2, 14, 9, 3, 10, 13, 15, 7, 11,
        ),
        (
            (), (69, 107, 118, 90), (), (48, 102, 116, 91, 77), (79,), (105,), (89,), (120, 88),
            (106,), (126, 33, 92), (110, 35, 94, 87, 121, 50, 124), (108, 85), (), (), (), (122,
            117, 103), (104, 51), (), (95, 125), (), (), (101, 93), (), (143, 109), (111, 135),
            (), (), (), (), (139,), (), (),
        ),
        (),
    ),
)


def live_weights(all_energy, batch_live, slots, total_slots, group_ids, frequencies, norm_factor):
    positions = jnp.arange(total_slots, dtype=jnp.int32)
    owner_match = (positions // slots)[:, None] == group_ids[None, :]
    limits = jnp.sum(jnp.where(owner_match, batch_live[None, :], 0), axis=1)
    is_live = (positions % slots < limits).astype(jnp.float32)
    weight = (
        -2.0
        * all_energy[None, :]
        / (all_energy[None, :] * all_energy[None, :] + frequencies[:, None] * frequencies[:, None])
    )
    return weight * is_live[None, :] * norm_factor


def plain_body(pair_density, energies, batch_live, coulomb_root):
    slots = pair_density.shape[0]
    width_own = pair_density.shape[1]
    group_count = lax.axis_size("grp")
    block_count = lax.axis_size("blk")
    total_slots = slots * group_count
    group_index = lax.axis_index("grp")
    block_index = lax.axis_index("blk")
    norm_factor = 1.0 / math.sqrt(total_slots)
    own_root = lax.dynamic_slice_in_dim(coulomb_root, block_index * width_own, width_own)
    group_ids = jnp.arange(group_count, dtype=jnp.int32)
    row_density, all_energy = (
        lax.all_gather(pair_density, "grp", axis=0, tiled=True),
        lax.all_gather(energies.astype(jnp.bfloat16), "grp", axis=0, tiled=True).astype(
            energies.dtype
        ),
    )
    frequencies = 0.6 * jnp.arange(group_count, dtype=jnp.float32)
    weight = live_weights(
        all_energy, batch_live, slots, total_slots, group_ids, frequencies, norm_factor
    )
    scaled = (weight[:, :, None] * row_density.astype(jnp.float32)[None, :, :]).astype(jnp.bfloat16)
    sub_width = width_own // group_count
    my_slice = lax.dynamic_slice_in_dim(row_density, group_index * sub_width, sub_width, 1)
    root_table = jnp.reshape(coulomb_root, (block_count, group_count, sub_width))
    my_roots = jnp.reshape(
        lax.dynamic_index_in_dim(root_table, group_index, 1, keepdims=False), (-1,)
    )
    chi = jnp.einsum(
        "ftc,tk->fck",
        scaled,
        lax.all_gather(my_slice, "blk", axis=1, tiled=True),
        preferred_element_type=jnp.float32,
    )
    quarter = own_root[None, :, None] * chi * my_roots[None, None, :]
    received = lax.all_to_all(
        quarter.astype(jnp.bfloat16), "grp", split_axis=0, concat_axis=0, tiled=True
    )
    received = jnp.reshape(received, (group_count, width_own, block_count, sub_width))
    polarized = jnp.reshape(
        jnp.transpose(received, (1, 2, 0, 3)), (width_own, width_own * block_count)
    )
    lead_blocks = (CW + width_own - 1) // width_own
    lead = quarter[:, :, : lead_blocks * sub_width]
    lead_back = lax.all_to_all(
        lead.astype(jnp.bfloat16), "grp", split_axis=0, concat_axis=0, tiled=True
    ).astype(lead.dtype)
    lead_back = jnp.reshape(lead_back, (group_count, width_own, lead_blocks, sub_width))
    window = jnp.reshape(
        jnp.transpose(lead_back, (1, 2, 0, 3)), (width_own, lead_blocks * width_own)
    )[:, :CW]
    state = window
    for dyson_step in range(DYSON):
        rounded = state.astype(jnp.bfloat16)
        product = jnp.dot(
            polarized,
            lax.all_gather(rounded, "blk", axis=0, tiled=True),
            preferred_element_type=jnp.float32,
        )
        state = window + 8.0 / G * product
    return (polarized[None], state[None])


def far_plane(z, nz, k):
    edge = jnp.minimum(z, nz - 1 - z)
    low = k if k > 1 else jnp.where(edge == 0, k, 1 - k)
    return jnp.where(2 * z < nz, low, nz - 1 - low)


def stream_kernel(
    rows_ref, energy_ref, live_ref, root_ref,
    out_ref, at_ref, m_ref, w_ref, lead_ref,
    p_ref, raw_ref, surplus_ref, spare_ref, energies_ref, column_ref, source_ref, scaled_ref,
    pick_a, pick_b, pick_s, stage_ref,
    recv, s_x, s_y, s_z, s_pair, s_local, s_raw, r_raw, s_sur, r_sur, s_energy, r_energy, s_out,
):
    g, b = lax.axis_index("grp"), lax.axis_index("blk")
    x, c = g // 2, g % 2
    z, y = b // 2, b % 2
    nz = p_ref.shape[0] // 2
    slots, width = rows_ref.shape
    packed, half = p_ref.shape[2], p_ref.shape[3]
    share, core = packed // 2, packed // 4
    first = (packed - 2 * slots) // 2
    second = core - first
    edge = jnp.minimum(z, nz - 1 - z)
    to_x = ((1 - x) * 2 + c, b)
    to_y = (g, z * 2 + 1 - y)
    to_pair = (x * 2 + 1 - c, b)
    inward = jnp.where(2 * z < nz, z + 1, z - 1)
    outward = 2 * z - inward
    to_in = (g, inward * 2 + y)
    to_out = (g, outward * 2 + y)
    middle = edge == 1

    barrier = pltpu.get_barrier_semaphore()

    def greet(to):
        pl.semaphore_signal(barrier, inc=1, device_id=to, device_id_type=MESH)

    keep_rows = [
        pltpu.make_async_copy(
            rows_ref.at[:, h * half:(h + 1) * half],
            raw_ref.at[c, :, h * half:(h + 1) * half], s_local.at[h])
        for h in range(2)
    ]
    keep_energy = pltpu.make_async_copy(energy_ref.at[0], energies_ref.at[g], s_local.at[2])
    for copy in keep_rows:
        copy.start()
    keep_energy.start()
    for to in (to_x, to_y, to_pair, to_in):
        greet(to)
    pl.when(middle)(lambda: greet(to_out))
    pl.semaphore_wait(barrier, 4 + middle.astype(jnp.int32))

    def rows_pair(h, who):
        return pltpu.make_async_remote_copy(
            src_ref=rows_ref.at[:, h * half:(h + 1) * half],
            dst_ref=raw_ref.at[who, :, h * half:(h + 1) * half],
            send_sem=s_raw.at[h], recv_sem=r_raw.at[h], device_id=to_pair, device_id_type=MESH)

    def energy_to(way, to, who):
        return pltpu.make_async_remote_copy(
            src_ref=energies_ref.at[who] if way == 2 else energy_ref.at[0],
            dst_ref=energies_ref.at[who], send_sem=s_energy.at[way], recv_sem=r_energy.at[who],
            device_id=to, device_id_type=MESH)

    g_x, g_pair, g_far = (1 - x) * 2 + c, x * 2 + 1 - c, (1 - x) * 2 + 1 - c
    for h in range(2):
        rows_pair(h, c).start()
    energy_to(0, to_x, g).start()
    energy_to(1, to_pair, g).start()

    live0, live1 = live_ref[2 * x], live_ref[2 * x + 1]
    count = live0 + live1

    def one_hot(ref, source):
        at = lax.broadcasted_iota(jnp.int32, ref.shape, 1)
        ref[...] = (source == at).astype(jnp.float32).astype(jnp.bfloat16)

    def column_iota(size):
        return lax.broadcasted_iota(jnp.int32, (size, 1), 0)

    position = column_iota(pick_s.shape[0]) + (share + c * pick_s.shape[0])
    one_hot(pick_s, jnp.where(position < count, position - live0, -1))
    slot = column_iota(first) + c * first
    one_hot(pick_a, jnp.where(slot < live0, slot, slots + slot - live0))
    slot = column_iota(second) + (2 * first + c * second)
    one_hot(pick_b, jnp.where(
        slot < live0, slot,
        jnp.where(slot < count, slots + slot - live0, 2 * slots + slot - count)))

    def item(ox, ob, cc, kind, h):
        start = ox * share + cc * core + (first if kind else 0)
        size = second if kind else first
        return p_ref.at[ob, h, pl.ds(pl.multiple_of(start, 64), size)]

    def send(ox, ob, p, sem, to, cc=None, h=None):
        cc = c if cc is None else cc
        kind, h = (p // 2, p % 2) if h is None else (p, h)
        ref = item(ox, ob, cc, kind, h)
        return pltpu.make_async_remote_copy(
            src_ref=ref, dst_ref=ref, send_sem=sem, recv_sem=recv.at[ox, ob, cc, kind * 2 + h],
            device_id=to, device_id_type=MESH)

    def over_x(ox, ob, p):
        return send(ox, ob, p, s_x.at[ob, p], to_x)

    def over_y(ox, ob, p):
        return send(ox, ob, p, s_y.at[ox, ob // 2, p], to_y)

    def over_in(ox, ob, p):
        return send(ox, ob, p, s_z.at[0, ox, ob // 2, p], to_in)

    def over_out(ox, ob, p):
        return send(ox, ob, p, s_z.at[1, ox, ob // 2, p], to_out)

    def onward(ox, zz, ob, p):
        low = zz < z
        to = (g, jnp.where(low, z + 1, z - 1) * 2 + y)
        way = jnp.where(low == (2 * z < nz), 0, 1)
        return send(ox, ob, p, s_z.at[way, ox, zz, p], to)

    def over_pair(ox, ob, p):
        return send(ox, ob, p, s_pair.at[ox, ob, p], to_pair)

    def surplus_x(h):
        return pltpu.make_async_remote_copy(
            src_ref=spare_ref.at[h], dst_ref=surplus_ref.at[h, c], send_sem=s_sur.at[0, h],
            recv_sem=r_sur.at[h, c], device_id=to_x, device_id_type=MESH)

    def surplus_pair(h, who):
        return pltpu.make_async_remote_copy(
            src_ref=surplus_ref.at[h, who], dst_ref=surplus_ref.at[h, who],
            send_sem=s_sur.at[1, h], recv_sem=r_sur.at[h, who], device_id=to_pair,
            device_id_type=MESH)

    def dot(left, right):
        return jnp.dot(left, right, preferred_element_type=jnp.float32)

    def raw(who, h):
        return raw_ref[who, :, h * half:(h + 1) * half]

    def fill(kind, h, value):
        start = pl.multiple_of(x * share + c * core + (first if kind else 0), 64)
        p_ref[b, h, pl.ds(start, second if kind else first)] = value.astype(jnp.bfloat16)

    for h in range(2):
        keep_rows[h].wait()
        rows_pair(h, 1 - c).wait_recv()
        spare_ref[h] = dot(pick_s[...], raw(1, h)).astype(jnp.bfloat16)
        surplus_x(h).start()
    for h in range(2):
        fill(0, h, dot(pick_a[:, :slots], raw(0, h)) + dot(pick_a[:, slots:], raw(1, h)))

    def prepare(h):
        surplus_x(h).wait_recv()
        surplus_pair(h, c).start()
        value = dot(pick_b[:, :slots], raw(0, h)) + dot(pick_b[:, slots:2 * slots], raw(1, h))
        surplus_pair(h, 1 - c).wait_recv()
        tail = pick_b.shape[1] - 2 * slots
        value += dot(pick_b[:, 2 * slots:2 * slots + tail // 2], surplus_ref[h, 0])
        fill(1, h, value + dot(pick_b[:, 2 * slots + tail // 2:], surplus_ref[h, 1]))

    def event(code):
        t, k, p = code // 16, code // 4 % 4, code % 4
        zz = far_plane(z, nz, k) if k else z
        ox = x if t in (OWN, YO, ZN, YN) else 1 - x
        ob = zz * 2 + (y if t in (OWN, XO, ZN, XN) else 1 - y)
        if t == OWN:
            if p >= 2:
                prepare(p % 2)
        else:
            send(ox, ob, p, s_pair.at[ox, ob, p], to_pair).wait_recv()
        return moves(t, k, p, zz, ox, ob, "start")

    def moves(t, k, p, zz, ox, ob, act):
        def do(make):
            getattr(make(), act)()

        if t in (OWN, ZN):
            if t == ZN:
                pl.when(middle)(lambda: do(lambda: onward(ox, zz, ob, p)))
            else:
                do(lambda: over_in(ox, ob, p))
                pl.when(middle)(lambda: do(lambda: over_out(ox, ob, p)))
            do(lambda: over_y(ox, ob, p))
            do(lambda: over_x(ox, ob, p))
        elif t == ZD:
            pl.when(middle)(lambda: do(lambda: onward(ox, zz, ob, p)))
        elif t == XO:
            do(lambda: over_y(ox, ob, p))
        elif t == YD and p < 3:
            do(lambda: over_in(ox, ob, p))
            pl.when(middle)(lambda: do(lambda: over_out(ox, ob, p)))
        elif t == XN and p == 3 and k in RELAY_Y:
            do(lambda: over_y(ox, ob, p))
        elif t == YN and p == 3 and k not in RELAY_Y:
            do(lambda: over_x(ox, ob, p))
        do(lambda: over_pair(ox, ob, p))

    def run(plans):
        for kind, codes in enumerate(plans):
            if codes:
                @pl.when(edge == kind)
                def _():
                    for code in codes:
                        event(code)

    def weights():
        energy_to(0, to_x, g_x).wait_recv()
        energy_to(2, to_pair, g_x).start()
        keep_energy.wait()
        energy_to(1, to_pair, g_pair).wait_recv()
        energy_to(2, to_pair, g_far).wait_recv()
        for k in range(4):
            column_ref[k * slots:(k + 1) * slots] = jnp.broadcast_to(
                energies_ref[k], (LANES, slots)).T
        row = lax.broadcasted_iota(jnp.int32, (1, packed), 1)
        upper = row >= share
        row = row - jnp.where(upper, share, 0)
        other = row >= core
        row = row - jnp.where(other, core, 0)
        late = row >= first
        row = row + jnp.where(
            late, 2 * first - first + jnp.where(other, second, 0), jnp.where(other, first, 0))
        a0, a1, a2, a3 = (live_ref[k] for k in range(4))
        n0 = jnp.where(upper, a2, a0)
        n1 = n0 + jnp.where(upper, a3, a1)
        base = jnp.where(upper, 2 * slots, 0)
        across = jnp.where(upper, slots - a0, 3 * slots - a2) + share
        source_ref[...] = jnp.where(
            row < n0, base + row,
            jnp.where(row < n1, base + slots + row - n0, across + row - n1))

        @pl.loop(0, packed // LANES)
        def _(k):
            part = pl.ds(pl.multiple_of(k * LANES, LANES), LANES)
            hit = source_ref[:, part] == lax.broadcasted_iota(
                jnp.int32, (4 * slots, LANES), 0)
            w_ref[:, part] = jnp.sum(
                jnp.where(hit, column_ref[...], 0.0), axis=0, keepdims=True)

        energy = w_ref[...]
        frequency = 0.6 * g.astype(jnp.float32)
        w_ref[...] = -2.0 * energy / (energy * energy + frequency * frequency) * (
            1.0 / math.sqrt(4 * slots))

    m_ref[...] = jnp.zeros_like(m_ref)
    leading = [plan[0] for plan in PLANS]
    early = [codes[:2] for codes in leading]
    run(early)
    weights()
    run([codes[2:] for codes in leading])

    def from_pair(ox, ob, kind, h):
        send(ox, ob, kind, s_pair.at[ox, ob, kind * 2 + h], to_pair, cc=1 - c, h=h).wait_recv()

    def ready(ob, h):
        for ox in range(2):
            for kind in range(2):
                from_pair(ox, ob, kind, h)

    for h in range(2):
        ready(b, h)
        for k in range(2):
            part = slice(k * half // 2, (k + 1) * half // 2)
            start = pl.multiple_of(b * width + h * half + k * (half // 2), half // 2)
            own = p_ref[b, h, :, part].astype(jnp.float32) * root_ref[:, pl.ds(start, half // 2)]
            rows = slice(h * half + part.start, h * half + part.stop)
            at_ref[rows] = (own.T * w_ref[...]).astype(jnp.bfloat16)

    units = 4 * nz

    def put(ob, h, lane):
        return pltpu.make_async_copy(stage_ref.at[lane], out_ref.at[ob, h], s_out.at[lane])

    @pl.loop(0, units)
    def _(step):
        def pick(table):
            value = table[0]
            for k in range(1, units):
                value = jnp.where(step == k, table[k], value)
            return value

        unit = jnp.where(edge == 0, pick(PLANS[0][1]), pick(PLANS[1][1]))
        k, other, h = unit // 4, unit // 2 % 2, unit % 2
        zz = z
        for j in range(1, nz):
            zz = jnp.where(k == j, far_plane(z, nz, j), zz)
        ob = zz * 2 + jnp.where(other == 1, 1 - y, y)
        root = root_ref[:, pl.ds(pl.multiple_of(ob * width + h * half, half), half)]

        def slot_events(which):
            for s in range(units):
                codes = [plan[2][2 * s + which] for plan in PLANS]
                if any(codes):
                    @pl.when(step == s)
                    def _():
                        run(codes)

        slot_events(0)

        @pl.when(unit >= 2)
        def _():
            ready(ob, h)

        lane = step % 2

        @pl.when(step >= 2)
        def _():
            put(ob, h, lane).wait()

        stage_ref[lane] = (dot(at_ref[...], p_ref[ob, h]) * root).astype(jnp.bfloat16)
        put(ob, h, lane).start()
        slot_events(1)
        scaled_ref[...] = (p_ref[ob, h].astype(jnp.float32) * (root * root)).astype(jnp.bfloat16)
        for a in range(0, packed, 256):
            m_ref[a:a + 256, a:] += lax.dot_general(
                scaled_ref[a:a + 256], p_ref[ob, h, a:], (((1,), (1,)), ((), ())),
                preferred_element_type=jnp.float32)

    run([plan[3] for plan in PLANS])
    lead_ref[...] = p_ref[0, 0, :, :CW]
    for lane in range(2):
        put(b, 0, lane).wait()

    energy_to(0, to_x, g).wait_send()
    energy_to(1, to_pair, g).wait_send()
    energy_to(2, to_pair, g_x).wait_send()
    for h in range(2):
        rows_pair(h, c).wait_send()
        surplus_x(h).wait_send()
        surplus_pair(h, c).wait_send()
    for code in EVENTS:
        t, k, p = code // 16, code // 4 % 4, code % 4
        zz = far_plane(z, nz, k) if k else z
        ox = x if t in (OWN, YO, ZN, YN) else 1 - x
        ob = zz * 2 + (y if t in (OWN, XO, ZN, XN) else 1 - y)
        moves(t, k, p, zz, ox, ob, "wait_send")


def stream(pair_density, energies, batch_live, coulomb_root, blocks):
    slots, width = pair_density.shape
    packed = slots * 5 // 2
    half = width // 2
    first = (packed - 2 * slots) // 2
    second = packed // 4 - first
    spare = (2 * slots - packed // 2) // 2
    nz = blocks // 2
    dma = pltpu.SemaphoreType.DMA
    vmem = pl.BlockSpec(memory_space=pltpu.VMEM)
    bf16, f32 = jnp.bfloat16, jnp.float32
    shape = jax.ShapeDtypeStruct
    return pl.pallas_call(
        stream_kernel,
        out_shape=(
            shape((blocks, 2, width, half), bf16),
            shape((width, packed), bf16),
            shape((packed, packed), f32),
            shape((1, packed), f32),
            shape((packed, CW), bf16),
        ),
        in_specs=[
            pl.BlockSpec(memory_space=pl.ANY), vmem,
            pl.BlockSpec(memory_space=pltpu.SMEM), vmem,
        ],
        out_specs=(pl.BlockSpec(memory_space=pl.ANY),) + (vmem,) * 4,
        scratch_shapes=[
            pltpu.VMEM((blocks, 2, packed, half), bf16),
            pltpu.VMEM((2, slots, width), bf16),
            pltpu.VMEM((2, 2, spare, half), bf16),
            pltpu.VMEM((2, spare, half), bf16),
            pltpu.VMEM((4, 1, slots), f32),
            pltpu.VMEM((4 * slots, LANES), f32),
            pltpu.VMEM((1, packed), jnp.int32),
            pltpu.VMEM((packed, half), bf16),
            pltpu.VMEM((first, 2 * slots), bf16),
            pltpu.VMEM((second, 2 * slots + 2 * spare), bf16),
            pltpu.VMEM((spare, slots), bf16),
            pltpu.VMEM((2, width, half), bf16),
            dma((2, blocks, 2, 4)), dma((blocks, 4)), dma((2, nz, 4)), dma((2, 2, nz, 4)),
            dma((2, blocks, 4)), dma((3,)), dma((2,)), dma((2,)), dma((2, 2)), dma((2, 2)),
            dma((3,)), dma((4,)), dma((2,)),
        ],
        compiler_params=pltpu.CompilerParams(
            collective_id=0, has_side_effects=True, vmem_limit_bytes=VMEM_LIMIT),
    )(pair_density, energies[None, None, :], batch_live, coulomb_root[None, :])


def finish_kernel(
    factor, out_ref, at_ref, m_ref, w_ref, lead_ref, root_ref, polar_ref, screen_ref,
    round_ref, hold_ref, s_in, s_out,
):
    blocks, halves, _, half = out_ref.shape
    units = range(blocks * halves)
    takes = [
        pltpu.make_async_copy(
            out_ref.at[k // halves, k % halves], hold_ref.at[k], s_in.at[k]) for k in units
    ]
    puts = [
        pltpu.make_async_copy(
            hold_ref.at[k], polar_ref.at[:, k * half:(k + 1) * half], s_out.at[k]) for k in units
    ]
    for copy in takes:
        copy.start()

    def pass_on(some):
        for k in some:
            takes[k].wait()
            puts[k].start()
    packed = m_ref.shape[0]
    tile = 256
    for a in range(0, packed, tile):
        round_ref[a:a + tile, a:] = m_ref[a:a + tile, a:].astype(jnp.bfloat16)

    def apply(v):
        parts = []
        for a in range(0, packed, tile):
            e = a + tile
            part = jnp.dot(v[:, :e], round_ref[:e, a:e], preferred_element_type=jnp.float32)
            if e < packed:
                part += lax.dot_general(
                    v[:, e:], round_ref[a:e, e:], (((1,), (1,)), ((), ())),
                    preferred_element_type=jnp.float32)
            parts.append(part)
        return jnp.concatenate(parts, axis=1)

    cut = len(units) // 4
    pass_on(units[:cut])
    w = w_ref[...]
    q = (lead_ref[...].astype(jnp.float32) * root_ref[:, :CW]).T
    u = apply((q * w).astype(jnp.bfloat16))
    pass_on(units[cut:2 * cut])
    u += apply((u * (w * factor)).astype(jnp.bfloat16))
    pass_on(units[2 * cut:3 * cut])
    last = (q + factor * u).astype(jnp.bfloat16)
    screen_ref[...] = lax.dot_general(
        at_ref[...], last, (((1,), (1,)), ((), ())), preferred_element_type=jnp.float32)
    pass_on(units[3 * cut:])
    for copy in puts:
        copy.wait()


def finish(out, at, m, w, lead, coulomb_root):
    blocks, halves, width, half = out.shape
    packed = at.shape[1]
    vmem = pl.BlockSpec(memory_space=pltpu.VMEM)
    return pl.pallas_call(
        functools.partial(finish_kernel, 8.0 / G),
        out_shape=(
            jax.ShapeDtypeStruct((width, blocks * halves * half), jnp.bfloat16),
            jax.ShapeDtypeStruct((width, CW), jnp.float32),
        ),
        in_specs=[pl.BlockSpec(memory_space=pl.ANY)] + [vmem] * 5,
        out_specs=(pl.BlockSpec(memory_space=pl.ANY), vmem),
        scratch_shapes=[
            pltpu.VMEM((packed, packed), jnp.bfloat16),
            pltpu.VMEM((blocks * halves, width, half), jnp.bfloat16),
            pltpu.SemaphoreType.DMA((blocks * halves,)),
            pltpu.SemaphoreType.DMA((blocks * halves,)),
        ],
        compiler_params=pltpu.CompilerParams(vmem_limit_bytes=FINISH_LIMIT),
    )(out, at, m, w, lead, coulomb_root[None, :])


def body(pair_density, energies, batch_live, coulomb_root):
    blocks = lax.axis_size("blk")
    out, at, m, w, lead = stream(pair_density, energies, batch_live, coulomb_root, blocks)
    polarized, screened = finish(out, at, m, w, lead, coulomb_root)
    return (polarized[None], screened[None])


def solution(mesh):
    placed = (P("grp", "blk"), P("grp"), P(), P())
    aligned = (
        mesh.shape["grp"] == 4
        and mesh.shape["blk"] == 8
        and (G // mesh.shape["blk"]) % (LANES * 8) == 0
    )
    return jax.shard_map(
        body if aligned else plain_body,
        mesh=mesh,
        in_specs=placed,
        out_specs=(P("grp", "blk", None), P("grp", "blk", None)),
        check_vma=False,
    )
```

time: 181 us -> 126 us (0.70); the launches traced: 179 us -> 126 us
  Pallas kernels: 172 us -> 122 us
  other arithmetic: 3.18 us -> 0 us
    pallas_call x2, Pallas kernels: 172 us -> 122 us  [the longest x1 110 us: stream(): pl.pallas_call(stream_kernel, out_shape=(shape((blocks, 2, width, half),...]
where the time goes in v1:
time: 126 us
  Pallas kernels  122 us (97%)
  local copies, waits for them, and re-layouts  3.31 us (3%)
    pallas_call x1, Pallas kernels, stream(): pl.pallas_call(stream_kernel, out_shape=(shape((blocks, 2, width, half),...  110 us
    pallas_call x1, Pallas kernels, finish(): pl.pallas_call(functools.partial(finish_kernel, 8.0 / G), out_shape=(jax....  12.2 us
    unnamed x8, local copies, waits for them, and re-layouts  3.31 us

profile of v1, /device:TPU:0, one launch (start us, length us, event | category | flops | bytes accessed | tf_op | source)
XLA Modules:
  0.0 126.2 jit_solution(114102161444421796)
XLA Ops:
  0.6 0.0 copy-start
  0.6 1.2 copy-done
  1.9 0.0 copy-start.1
  1.9 0.8 copy-done.1
  2.6 0.0 copy-start.2
  2.6 0.7 copy-done.2
  3.3 0.0 copy-start.3
  3.3 0.7 copy-done.3
  4.0 109.9 %shard_map.59 = (bf16[8,2,1024,512]{3,2,1,0:T(8,128)(2,1)}, bf16[1024,1280]{1,0:T(8,128)(2,1)S(1)}, f32[1280,1280]{1,0:T(8,128)S(1)}, f32[1,1280]{1,0:T(1,128)S(1)}, bf16[1280,128]{1,0:T(8,128)(2,1)S(1)}) custom-call(bf16[512,1024]{1,0:T(8,128)(2,1)S(1)} %copy-done, f32[1,1,512]{2,1,0:T(1,128)S(1)} %bitcast.6, s32[4]{0:T(128)S(1)} %copy-done.3, ...), custom_call_target="tpu_custom_call" | custom-call | tf_op jit(solution)/shard_map/pallas_call | solution.py:488
  113.8 12.2 %shard_map.60 = (bf16[1024,8192]{1,0:T(8,128)(2,1)}, f32[1024,128]{1,0:T(8,128)}) custom-call(bf16[8,2,1024,512]{3,2,1,0:T(8,128)(2,1)} %get-tuple-element.9.out_ref, bf16[1024,1280]{1,0:T(8,128)(2,1)S(1)} %get-tuple-element.10.at_ref, f32[1280,1280]{1,0:T(8,128)S(1)} %get-tuple-element.11.m_ref, f32[1,1280]{1,0:T(1,128)S(1)} %get-tuple-element.12.w_ref, ...), custom_call_target="tpu_custom_call" | custom-call | tf_op jit(solution)/shard_map/pallas_call | solution.py:582
Async XLA Ops:
  0.6 1.2 copy-start
  1.9 0.8 copy-start.1
  2.6 0.7 copy-start.2
  3.3 0.7 copy-start.3

commit v2 on v1

--- a/solution.py
+++ b/solution.py
@@ -13,10 +13,10 @@
 DYSON = 2
 LANES = 128
 MESH = pl.DeviceIdType.MESH
-VMEM_LIMIT = 34 * 1024 * 1024
-FINISH_LIMIT = 30 * 1024 * 1024
+VMEM_LIMIT = 30 * 1024 * 1024
+FINISH_LIMIT = 10 * 1024 * 1024
 OWN, XO, YO, YD, ZN, XN, YN, ZD, RD = range(9)
-RELAY_Y = (3,)
+RELAY_Y = (2,)
 EVENTS = (
     0, 1, 2, 3, 16, 17, 18, 19, 32, 33, 34, 35, 48, 49, 50, 51, 68, 69, 70, 71, 72, 73, 74,
     75, 76, 77, 78, 79, 84, 85, 86, 87, 88, 89, 90, 91, 92, 93, 94, 95, 100, 101, 102, 103,
@@ -26,32 +26,31 @@
 PLANS = (
     (
         (
-            0, 69, 2, 3, 71, 18, 1, 50, 32, 16, 68, 76, 70, 73, 19, 17, 85, 87, 84, 34, 75,
+            0, 1, 68, 32, 2, 3, 16, 69, 18, 84, 19, 17, 50, 71, 34, 70, 48,
         ),
         (
-            1, 0, 5, 2, 4, 12, 3, 8, 13, 9, 11, 7, 15, 10, 14, 6,
+            2, 1, 0, 4, 5, 3, 7, 12, 13, 6, 9, 14, 11, 15, 10, 8,
         ),
         (
-            (108, 92, 48), (), (), (101, 72), (), (33, 35, 105, 78, 86, 74), (89,), (), (49,
-            117, 100, 102), (77, 94, 51), (), (116,), (79, 90, 88, 126), (104,), (107, 91), (93,
-            103, 95), (), (), (109, 118, 139), (110, 121), (122,), (135,), (), (106, 143, 125,
-            111), (120,), (), (), (124,), (), (), (), (),
+            (), (101,), (76,), (), (85,), (51, 49), (35, 86, 87, 103), (92, 102, 33, 117, 78),
+            (), (79,), (), (135, 108, 77, 94), (), (75, 95), (), (93, 73, 116), (), (100, 118,
+            111, 91, 72), (), (89, 107), (110, 74), (124, 126), (105, 143), (109, 125, 139,
+            121), (120, 104), (), (), (122, 106, 90, 88), (), (), (), (),
         ),
         (),
     ),
     (
         (
-            1, 0, 2, 17, 3, 70, 68, 74, 73, 75, 16, 76, 84, 72, 86, 49, 18, 34, 32, 78, 100, 19,
-            71,
+            0, 1, 68, 2, 3, 16, 17, 70, 74, 76, 72, 19, 84, 18, 78, 75, 69, 71, 73, 102,
         ),
         (
-            0, 4, 1, 6, 8, 12, 5, 2, 14, 9, 3, 10, 13, 15, 7, 11,
+            0, 1, 4, 6, 3, 8, 2, 12, 14, 10, 9, 13, 7, 5, 11, 15,
         ),
         (
-            (), (69, 107, 118, 90), (), (48, 102, 116, 91, 77), (79,), (105,), (89,), (120, 88),
-            (106,), (126, 33, 92), (110, 35, 94, 87, 121, 50, 124), (108, 85), (), (), (), (122,
-            117, 103), (104, 51), (), (95, 125), (), (), (101, 93), (), (143, 109), (111, 135),
-            (), (), (), (), (139,), (), (),
+            (), (86,), (49, 100, 79, 116), (90, 118, 34), (77, 35), (33, 88), (117,), (104, 51,
+            48), (), (32,), (126, 108, 92, 50, 94), (110,), (124, 91), (), (), (121, 101, 106,
+            125, 120), (89, 107, 122, 85), (), (), (103, 87, 95), (), (93, 105), (), (135,),
+            (111, 109), (), (), (139,), (143,), (), (), (),
         ),
         (),
     ),
@@ -141,11 +140,11 @@
 
 
 def stream_kernel(
-    rows_ref, energy_ref, live_ref, root_ref,
-    out_ref, at_ref, m_ref, w_ref, lead_ref,
-    p_ref, raw_ref, surplus_ref, spare_ref, energies_ref, column_ref, source_ref, scaled_ref,
-    pick_a, pick_b, pick_s, stage_ref,
-    recv, s_x, s_y, s_z, s_pair, s_local, s_raw, r_raw, s_sur, r_sur, s_energy, r_energy, s_out,
+    rows_ref, energy_ref, lives_ref, roots_ref,
+    low_ref, high_ref, at_ref, m_ref, w_ref, lead_ref,
+    p_ref, raw_ref, surplus_ref, spare_ref, energies_ref, column_ref, source_ref,
+    pick_a, pick_b, pick_s, live_ref, root_ref,
+    recv, s_x, s_y, s_z, s_pair, s_local, s_raw, r_raw, s_sur, r_sur, s_energy, r_energy,
 ):
     g, b = lax.axis_index("grp"), lax.axis_index("blk")
     x, c = g // 2, g % 2
@@ -178,9 +177,13 @@
         for h in range(2)
     ]
     keep_energy = pltpu.make_async_copy(energy_ref.at[0], energies_ref.at[g], s_local.at[2])
+    keep_live = pltpu.make_async_copy(lives_ref, live_ref, s_local.at[3])
+    keep_root = pltpu.make_async_copy(roots_ref, root_ref, s_local.at[4])
+    keep_live.start()
     for copy in keep_rows:
         copy.start()
     keep_energy.start()
+    keep_root.start()
     for to in (to_x, to_y, to_pair, to_in):
         greet(to)
     pl.when(middle)(lambda: greet(to_out))
@@ -204,6 +207,7 @@
     energy_to(0, to_x, g).start()
     energy_to(1, to_pair, g).start()
 
+    keep_live.wait()
     live0, live1 = live_ref[2 * x], live_ref[2 * x + 1]
     count = live0 + live1
 
@@ -276,6 +280,7 @@
 
     def fill(kind, h, value):
         start = pl.multiple_of(x * share + c * core + (first if kind else 0), 64)
+        value = value * root_ref[:, pl.ds(pl.multiple_of(b * width + h * half, half), half)]
         p_ref[b, h, pl.ds(start, second if kind else first)] = value.astype(jnp.bfloat16)
 
     for h in range(2):
@@ -283,6 +288,7 @@
         rows_pair(h, 1 - c).wait_recv()
         spare_ref[h] = dot(pick_s[...], raw(1, h)).astype(jnp.bfloat16)
         surplus_x(h).start()
+    keep_root.wait()
     for h in range(2):
         fill(0, h, dot(pick_a[:, :slots], raw(0, h)) + dot(pick_a[:, slots:], raw(1, h)))
 
@@ -398,15 +404,11 @@
         ready(b, h)
         for k in range(2):
             part = slice(k * half // 2, (k + 1) * half // 2)
-            start = pl.multiple_of(b * width + h * half + k * (half // 2), half // 2)
-            own = p_ref[b, h, :, part].astype(jnp.float32) * root_ref[:, pl.ds(start, half // 2)]
+            own = p_ref[b, h, :, part].astype(jnp.float32)
             rows = slice(h * half + part.start, h * half + part.stop)
             at_ref[rows] = (own.T * w_ref[...]).astype(jnp.bfloat16)
 
     units = 4 * nz
-
-    def put(ob, h, lane):
-        return pltpu.make_async_copy(stage_ref.at[lane], out_ref.at[ob, h], s_out.at[lane])
 
     @pl.loop(0, units)
     def _(step):
@@ -422,7 +424,6 @@
         for j in range(1, nz):
             zz = jnp.where(k == j, far_plane(z, nz, j), zz)
         ob = zz * 2 + jnp.where(other == 1, 1 - y, y)
-        root = root_ref[:, pl.ds(pl.multiple_of(ob * width + h * half, half), half)]
 
         def slot_events(which):
             for s in range(units):
@@ -438,25 +439,19 @@
         def _():
             ready(ob, h)
 
-        lane = step % 2
-
-        @pl.when(step >= 2)
-        def _():
-            put(ob, h, lane).wait()
-
-        stage_ref[lane] = (dot(at_ref[...], p_ref[ob, h]) * root).astype(jnp.bfloat16)
-        put(ob, h, lane).start()
+        for first_block, tiles in ((0, low_ref), (nz, high_ref)):
+            @pl.when(ob // nz == first_block // nz)
+            def _():
+                tiles[ob - first_block, h] = dot(at_ref[...], p_ref[ob, h]).astype(jnp.bfloat16)
+
         slot_events(1)
-        scaled_ref[...] = (p_ref[ob, h].astype(jnp.float32) * (root * root)).astype(jnp.bfloat16)
         for a in range(0, packed, 256):
             m_ref[a:a + 256, a:] += lax.dot_general(
-                scaled_ref[a:a + 256], p_ref[ob, h, a:], (((1,), (1,)), ((), ())),
+                p_ref[ob, h, a:a + 256], p_ref[ob, h, a:], (((1,), (1,)), ((), ())),
                 preferred_element_type=jnp.float32)
 
     run([plan[3] for plan in PLANS])
     lead_ref[...] = p_ref[0, 0, :, :CW]
-    for lane in range(2):
-        put(b, 0, lane).wait()
 
     energy_to(0, to_x, g).wait_send()
     energy_to(1, to_pair, g).wait_send()
@@ -484,21 +479,18 @@
     dma = pltpu.SemaphoreType.DMA
     vmem = pl.BlockSpec(memory_space=pltpu.VMEM)
     bf16, f32 = jnp.bfloat16, jnp.float32
-    shape = jax.ShapeDtypeStruct
     return pl.pallas_call(
         stream_kernel,
         out_shape=(
-            shape((blocks, 2, width, half), bf16),
-            shape((width, packed), bf16),
-            shape((packed, packed), f32),
-            shape((1, packed), f32),
-            shape((packed, CW), bf16),
-        ),
-        in_specs=[
-            pl.BlockSpec(memory_space=pl.ANY), vmem,
-            pl.BlockSpec(memory_space=pltpu.SMEM), vmem,
-        ],
-        out_specs=(pl.BlockSpec(memory_space=pl.ANY),) + (vmem,) * 4,
+            pltpu.VMEM((nz, 2, width, half), bf16),
+            pltpu.VMEM((nz, 2, width, half), bf16),
+            pltpu.VMEM((width, packed), bf16),
+            pltpu.VMEM((packed, packed), f32),
+            pltpu.VMEM((1, packed), f32),
+            pltpu.VMEM((packed, CW), bf16),
+        ),
+        in_specs=[pl.BlockSpec(memory_space=pltpu.HBM)] * 4,
+        out_specs=(vmem,) * 6,
         scratch_shapes=[
             pltpu.VMEM((blocks, 2, packed, half), bf16),
             pltpu.VMEM((2, slots, width), bf16),
@@ -507,41 +499,35 @@
             pltpu.VMEM((4, 1, slots), f32),
             pltpu.VMEM((4 * slots, LANES), f32),
             pltpu.VMEM((1, packed), jnp.int32),
-            pltpu.VMEM((packed, half), bf16),
             pltpu.VMEM((first, 2 * slots), bf16),
             pltpu.VMEM((second, 2 * slots + 2 * spare), bf16),
             pltpu.VMEM((spare, slots), bf16),
-            pltpu.VMEM((2, width, half), bf16),
+            pltpu.SMEM((4,), jnp.int32),
+            pltpu.VMEM((1, coulomb_root.shape[0]), f32),
             dma((2, blocks, 2, 4)), dma((blocks, 4)), dma((2, nz, 4)), dma((2, 2, nz, 4)),
-            dma((2, blocks, 4)), dma((3,)), dma((2,)), dma((2,)), dma((2, 2)), dma((2, 2)),
-            dma((3,)), dma((4,)), dma((2,)),
+            dma((2, blocks, 4)), dma((5,)), dma((2,)), dma((2,)), dma((2, 2)), dma((2, 2)),
+            dma((3,)), dma((4,)),
         ],
         compiler_params=pltpu.CompilerParams(
             collective_id=0, has_side_effects=True, vmem_limit_bytes=VMEM_LIMIT),
-    )(pair_density, energies[None, None, :], batch_live, coulomb_root[None, :])
+    )(*(
+        pltpu.with_memory_space_constraint(value, pltpu.HBM)
+        for value in (pair_density, energies[None, None, :], batch_live, coulomb_root[None, :])
+    ))
 
 
 def finish_kernel(
-    factor, out_ref, at_ref, m_ref, w_ref, lead_ref, root_ref, polar_ref, screen_ref,
-    round_ref, hold_ref, s_in, s_out,
+    factor, low_ref, high_ref, at_ref, m_ref, w_ref, lead_ref, polar_ref, screen_ref,
+    round_ref, sems,
 ):
-    blocks, halves, _, half = out_ref.shape
-    units = range(blocks * halves)
-    takes = [
-        pltpu.make_async_copy(
-            out_ref.at[k // halves, k % halves], hold_ref.at[k], s_in.at[k]) for k in units
+    count, halves, _, half = low_ref.shape
+    tiles = [ref.at[k, h] for ref in (low_ref, high_ref) for k in range(count) for h in range(halves)]
+    copies = [
+        pltpu.make_async_copy(tile, polar_ref.at[:, k * half:(k + 1) * half], sems.at[k])
+        for k, tile in enumerate(tiles)
     ]
-    puts = [
-        pltpu.make_async_copy(
-            hold_ref.at[k], polar_ref.at[:, k * half:(k + 1) * half], s_out.at[k]) for k in units
-    ]
-    for copy in takes:
+    for copy in copies:
         copy.start()
-
-    def pass_on(some):
-        for k in some:
-            takes[k].wait()
-            puts[k].start()
     packed = m_ref.shape[0]
     tile = 256
     for a in range(0, packed, tile):
@@ -559,48 +545,45 @@
             parts.append(part)
         return jnp.concatenate(parts, axis=1)
 
-    cut = len(units) // 4
-    pass_on(units[:cut])
     w = w_ref[...]
-    q = (lead_ref[...].astype(jnp.float32) * root_ref[:, :CW]).T
+    q = lead_ref[...].astype(jnp.float32).T
     u = apply((q * w).astype(jnp.bfloat16))
-    pass_on(units[cut:2 * cut])
     u += apply((u * (w * factor)).astype(jnp.bfloat16))
-    pass_on(units[2 * cut:3 * cut])
     last = (q + factor * u).astype(jnp.bfloat16)
     screen_ref[...] = lax.dot_general(
         at_ref[...], last, (((1,), (1,)), ((), ())), preferred_element_type=jnp.float32)
-    pass_on(units[3 * cut:])
-    for copy in puts:
+    for copy in copies:
         copy.wait()
 
 
-def finish(out, at, m, w, lead, coulomb_root):
-    blocks, halves, width, half = out.shape
+def finish(low, high, at, m, w, lead):
+    count, halves, width, half = low.shape
+    units = 2 * count * halves
     packed = at.shape[1]
     vmem = pl.BlockSpec(memory_space=pltpu.VMEM)
     return pl.pallas_call(
         functools.partial(finish_kernel, 8.0 / G),
         out_shape=(
-            jax.ShapeDtypeStruct((width, blocks * halves * half), jnp.bfloat16),
+            jax.ShapeDtypeStruct((width, units * half), jnp.bfloat16),
             jax.ShapeDtypeStruct((width, CW), jnp.float32),
         ),
-        in_specs=[pl.BlockSpec(memory_space=pl.ANY)] + [vmem] * 5,
+        in_specs=[vmem] * 6,
         out_specs=(pl.BlockSpec(memory_space=pl.ANY), vmem),
         scratch_shapes=[
             pltpu.VMEM((packed, packed), jnp.bfloat16),
-            pltpu.VMEM((blocks * halves, width, half), jnp.bfloat16),
-            pltpu.SemaphoreType.DMA((blocks * halves,)),
-            pltpu.SemaphoreType.DMA((blocks * halves,)),
+            pltpu.SemaphoreType.DMA((units,)),
         ],
         compiler_params=pltpu.CompilerParams(vmem_limit_bytes=FINISH_LIMIT),
-    )(out, at, m, w, lead, coulomb_root[None, :])
+    )(*(
+        pltpu.with_memory_space_constraint(value, pltpu.VMEM)
+        for value in (low, high, at, m, w, lead)
+    ))
 
 
 def body(pair_density, energies, batch_live, coulomb_root):
     blocks = lax.axis_size("blk")
-    out, at, m, w, lead = stream(pair_density, energies, batch_live, coulomb_root, blocks)
-    polarized, screened = finish(out, at, m, w, lead, coulomb_root)
+    streamed = stream(pair_density, energies, batch_live, coulomb_root, blocks)
+    polarized, screened = finish(*streamed)
     return (polarized[None], screened[None])
 
 

time: 126 us -> 105 us (0.83)
  Pallas kernels: 122 us -> 104 us
  local copies, waits for them, and re-layouts: 3.31 us -> 0 us
    pallas_call x1, Pallas kernels: 110 us -> 96.2 us  [stream(): pl.pallas_call(stream_kernel, out_shape=(pltpu.VMEM((nz, 2, width, half),...]
    pallas_call x1, Pallas kernels: 12.2 us -> 7.85 us  [finish(): pl.pallas_call(functools.partial(finish_kernel, 8.0 / G), out_shape=(jax....]
    unnamed x8 -> x0, local copies, waits for them, and re-layouts: 3.31 us -> none
where the time goes in v2:
time: 105 us
  Pallas kernels  104 us (99%)
    pallas_call x1, Pallas kernels, stream(): pl.pallas_call(stream_kernel, out_shape=(pltpu.VMEM((nz, 2, width, half),...  96.2 us
    pallas_call x1, Pallas kernels, finish(): pl.pallas_call(functools.partial(finish_kernel, 8.0 / G), out_shape=(jax....  7.85 us

profile of v2, /device:TPU:0, one launch (start us, length us, event | category | flops | bytes accessed | tf_op | source)
XLA Modules:
  0.0 104.7 jit_solution(14739065860542411707)
XLA Ops:
  0.6 96.2 %shard_map.59 = (bf16[4,2,1024,512]{3,2,1,0:T(8,128)(2,1)S(1)}, bf16[4,2,1024,512]{3,2,1,0:T(8,128)(2,1)S(1)}, bf16[1024,1280]{1,0:T(8,128)(2,1)S(1)}, f32[1280,...) custom-call(bf16[512,1024]{1,0:T(8,128)(2,1)} %rows_ref.1, f32[1,1,512]{2,1,0:T(1,128)} %bitcast.5, ...), custom_call_target="tpu_custom_call" | custom-call | tf_op jit(solution)/shard_map/pallas_call | solution.py:482
  96.8 7.8 %shard_map.60 = (bf16[1024,8192]{1,0:T(8,128)(2,1)}, f32[1024,128]{1,0:T(8,128)}) custom-call(bf16[4,2,1024,512]{3,2,1,0:T(8,128)(2,1)S(1)} %get-tuple-element.10.low_ref, bf16[4,2,1024,512]{3,2,1,0:T(8,128)(2,1)S(1)} %get-tuple-element.11.high_ref, bf16[1024,1280]{1,0:T(8,128)(2,1)S(1)} %get-tuple-element.12.at_ref, ...), custom_call_target="tpu_custom_call" | custom-call | tf_op jit(solution)/shard_map/pallas_call | solution.py:564

commit v3 on v2

--- a/solution.py
+++ b/solution.py
@@ -139,12 +139,30 @@
     return jnp.where(2 * z < nz, low, nz - 1 - low)
 
 
+def place_of(step, units, edge, z, y, nz):
+    def pick(table):
+        if isinstance(step, int):
+            return table[step]
+        value = table[0]
+        for k in range(1, units):
+            value = jnp.where(step == k, table[k], value)
+        return value
+
+    unit = jnp.where(edge == 0, pick(PLANS[0][1]), pick(PLANS[1][1]))
+    k, other = unit // 4, unit // 2 % 2
+    zz = z
+    for j in range(1, nz):
+        zz = jnp.where(k == j, far_plane(z, nz, j), zz)
+    return zz * 2 + jnp.where(other == 1, 1 - y, y), unit % 2
+
+
 def stream_kernel(
     rows_ref, energy_ref, lives_ref, roots_ref,
-    low_ref, high_ref, at_ref, m_ref, w_ref, lead_ref,
+    tiles0_ref, tiles1_ref, tiles2_ref, tiles3_ref,
+    at_ref, m_ref, w_ref, lead_ref, late_ref,
     p_ref, raw_ref, surplus_ref, spare_ref, energies_ref, column_ref, source_ref,
     pick_a, pick_b, pick_s, live_ref, root_ref,
-    recv, s_x, s_y, s_z, s_pair, s_local, s_raw, r_raw, s_sur, r_sur, s_energy, r_energy,
+    recv, s_x, s_y, s_z, s_pair, s_local, s_raw, r_raw, s_sur, r_sur, s_energy, r_energy, s_late,
 ):
     g, b = lax.axis_index("grp"), lax.axis_index("blk")
     x, c = g // 2, g % 2
@@ -187,7 +205,6 @@
     for to in (to_x, to_y, to_pair, to_in):
         greet(to)
     pl.when(middle)(lambda: greet(to_out))
-    pl.semaphore_wait(barrier, 4 + middle.astype(jnp.int32))
 
     def rows_pair(h, who):
         return pltpu.make_async_remote_copy(
@@ -200,12 +217,6 @@
             src_ref=energies_ref.at[who] if way == 2 else energy_ref.at[0],
             dst_ref=energies_ref.at[who], send_sem=s_energy.at[way], recv_sem=r_energy.at[who],
             device_id=to, device_id_type=MESH)
-
-    g_x, g_pair, g_far = (1 - x) * 2 + c, x * 2 + 1 - c, (1 - x) * 2 + 1 - c
-    for h in range(2):
-        rows_pair(h, c).start()
-    energy_to(0, to_x, g).start()
-    energy_to(1, to_pair, g).start()
 
     keep_live.wait()
     live0, live1 = live_ref[2 * x], live_ref[2 * x + 1]
@@ -227,6 +238,15 @@
         slot < live0, slot,
         jnp.where(slot < count, slots + slot - live0, 2 * slots + slot - count)))
 
+    m_ref[...] = jnp.zeros_like(m_ref)
+    pl.semaphore_wait(barrier, 4 + middle.astype(jnp.int32))
+
+    g_x, g_pair, g_far = (1 - x) * 2 + c, x * 2 + 1 - c, (1 - x) * 2 + 1 - c
+    for h in range(2):
+        rows_pair(h, c).start()
+    energy_to(0, to_x, g).start()
+    energy_to(1, to_pair, g).start()
+
     def item(ox, ob, cc, kind, h):
         start = ox * share + cc * core + (first if kind else 0)
         size = second if kind else first
@@ -288,10 +308,6 @@
         rows_pair(h, 1 - c).wait_recv()
         spare_ref[h] = dot(pick_s[...], raw(1, h)).astype(jnp.bfloat16)
         surplus_x(h).start()
-    keep_root.wait()
-    for h in range(2):
-        fill(0, h, dot(pick_a[:, :slots], raw(0, h)) + dot(pick_a[:, slots:], raw(1, h)))
-
     def prepare(h):
         surplus_x(h).wait_recv()
         surplus_pair(h, c).start()
@@ -385,12 +401,12 @@
         w_ref[...] = -2.0 * energy / (energy * energy + frequency * frequency) * (
             1.0 / math.sqrt(4 * slots))
 
-    m_ref[...] = jnp.zeros_like(m_ref)
-    leading = [plan[0] for plan in PLANS]
-    early = [codes[:2] for codes in leading]
-    run(early)
+    keep_root.wait()
+    for h in range(2):
+        fill(0, h, dot(pick_a[:, :slots], raw(0, h)) + dot(pick_a[:, slots:], raw(1, h)))
+        event(h)
     weights()
-    run([codes[2:] for codes in leading])
+    run([[code for code in plan[0] if code not in (0, 1)] for plan in PLANS])
 
     def from_pair(ox, ob, kind, h):
         send(ox, ob, kind, s_pair.at[ox, ob, kind * 2 + h], to_pair, cc=1 - c, h=h).wait_recv()
@@ -410,49 +426,57 @@
 
     units = 4 * nz
 
-    @pl.loop(0, units)
+    def slot_events(s):
+        run([plan[2][s] for plan in PLANS])
+
+    @pl.loop(0, units - 1)
     def _(step):
-        def pick(table):
-            value = table[0]
-            for k in range(1, units):
-                value = jnp.where(step == k, table[k], value)
-            return value
-
-        unit = jnp.where(edge == 0, pick(PLANS[0][1]), pick(PLANS[1][1]))
-        k, other, h = unit // 4, unit // 2 % 2, unit % 2
-        zz = z
-        for j in range(1, nz):
-            zz = jnp.where(k == j, far_plane(z, nz, j), zz)
-        ob = zz * 2 + jnp.where(other == 1, 1 - y, y)
-
-        def slot_events(which):
-            for s in range(units):
-                codes = [plan[2][2 * s + which] for plan in PLANS]
-                if any(codes):
+        ob, h = place_of(step, units, edge, z, y, nz)
+
+        def events(which):
+            for s in range(units - 1):
+                if any(plan[2][2 * s + which] for plan in PLANS):
                     @pl.when(step == s)
                     def _():
-                        run(codes)
-
-        slot_events(0)
-
-        @pl.when(unit >= 2)
+                        slot_events(2 * s + which)
+
+        events(0)
+
+        @pl.when(ob != b)
         def _():
             ready(ob, h)
 
-        for first_block, tiles in ((0, low_ref), (nz, high_ref)):
-            @pl.when(ob // nz == first_block // nz)
+        for k, tiles in enumerate((tiles0_ref, tiles1_ref, tiles2_ref, tiles3_ref)):
+            count = tiles.shape[0]
+
+            @pl.when(ob // count == k)
             def _():
-                tiles[ob - first_block, h] = dot(at_ref[...], p_ref[ob, h]).astype(jnp.bfloat16)
-
-        slot_events(1)
-        for a in range(0, packed, 256):
-            m_ref[a:a + 256, a:] += lax.dot_general(
-                p_ref[ob, h, a:a + 256], p_ref[ob, h, a:], (((1,), (1,)), ((), ())),
-                preferred_element_type=jnp.float32)
-
+                tiles[ob - k * count, h] = dot(at_ref[...], p_ref[ob, h]).astype(jnp.bfloat16)
+
+        events(1)
+
+        @pl.when(step < units - 2)
+        def _():
+            for a in range(0, packed, 256):
+                m_ref[a:a + 256, a:] += lax.dot_general(
+                    p_ref[ob, h, a:a + 256], p_ref[ob, h, a:], (((1,), (1,)), ((), ())),
+                    preferred_element_type=jnp.float32)
+
+    def hand_on(k):
+        ob, h = place_of(units - 2 + k, units, edge, z, y, nz)
+        return pltpu.make_async_copy(p_ref.at[ob, h], late_ref.at[:, k * half:(k + 1) * half], s_late.at[k])
+
+    hand_on(0).start()
+    slot_events(2 * units - 2)
+    slot_events(2 * units - 1)
     run([plan[3] for plan in PLANS])
+    ob, h = place_of(units - 1, units, edge, z, y, nz)
+    ready(ob, h)
+    hand_on(1).start()
     lead_ref[...] = p_ref[0, 0, :, :CW]
 
+    for k in range(2):
+        hand_on(k).wait()
     energy_to(0, to_x, g).wait_send()
     energy_to(1, to_pair, g).wait_send()
     energy_to(2, to_pair, g_x).wait_send()
@@ -482,15 +506,15 @@
     return pl.pallas_call(
         stream_kernel,
         out_shape=(
-            pltpu.VMEM((nz, 2, width, half), bf16),
-            pltpu.VMEM((nz, 2, width, half), bf16),
+            *(pltpu.VMEM((nz // 2, 2, width, half), bf16),) * 4,
             pltpu.VMEM((width, packed), bf16),
             pltpu.VMEM((packed, packed), f32),
             pltpu.VMEM((1, packed), f32),
             pltpu.VMEM((packed, CW), bf16),
+            pltpu.VMEM((packed, 2 * half), bf16),
         ),
         in_specs=[pl.BlockSpec(memory_space=pltpu.HBM)] * 4,
-        out_specs=(vmem,) * 6,
+        out_specs=(vmem,) * 9,
         scratch_shapes=[
             pltpu.VMEM((blocks, 2, packed, half), bf16),
             pltpu.VMEM((2, slots, width), bf16),
@@ -506,7 +530,7 @@
             pltpu.VMEM((1, coulomb_root.shape[0]), f32),
             dma((2, blocks, 2, 4)), dma((blocks, 4)), dma((2, nz, 4)), dma((2, 2, nz, 4)),
             dma((2, blocks, 4)), dma((5,)), dma((2,)), dma((2,)), dma((2, 2)), dma((2, 2)),
-            dma((3,)), dma((4,)),
+            dma((3,)), dma((4,)), dma((2,)),
         ],
         compiler_params=pltpu.CompilerParams(
             collective_id=0, has_side_effects=True, vmem_limit_bytes=VMEM_LIMIT),
@@ -517,21 +541,43 @@
 
 
 def finish_kernel(
-    factor, low_ref, high_ref, at_ref, m_ref, w_ref, lead_ref, polar_ref, screen_ref,
-    round_ref, sems,
+    factor, tiles0_ref, tiles1_ref, tiles2_ref, tiles3_ref,
+    at_ref, m_ref, w_ref, lead_ref, late_ref, polar_ref, screen_ref,
+    round_ref, last_ref, v_ref, u_ref, sems,
 ):
-    count, halves, _, half = low_ref.shape
-    tiles = [ref.at[k, h] for ref in (low_ref, high_ref) for k in range(count) for h in range(halves)]
-    copies = [
-        pltpu.make_async_copy(tile, polar_ref.at[:, k * half:(k + 1) * half], sems.at[k])
-        for k, tile in enumerate(tiles)
-    ]
-    for copy in copies:
-        copy.start()
+    b = lax.axis_index("blk")
+    tiles = (tiles0_ref, tiles1_ref, tiles2_ref, tiles3_ref)
+    count, halves, _, half = tiles[0].shape
+    units = len(tiles) * count * halves
+    nz = units // (2 * halves)
+    z, y = b // 2, b % 2
+    ob, h = place_of(units - 1, units, jnp.minimum(z, nz - 1 - z), z, y, nz)
+    late = ob * halves + h
+
+    def copy(k):
+        return pltpu.make_async_copy(
+            tiles[k // (halves * count)].at[k // halves % count, k % halves],
+            polar_ref.at[:, k * half:(k + 1) * half], sems.at[k])
+
+    for k in range(units):
+        pl.when(late != k)(lambda k=k: copy(k).start())
+    tile = 256
+
+    @pl.loop(0, last_ref.shape[0] // tile)
+    def _(k):
+        rows = pl.ds(pl.multiple_of(k * tile, tile), tile)
+        last_ref[rows] = jnp.dot(
+            at_ref[rows], late_ref[:, half:], preferred_element_type=jnp.float32
+        ).astype(jnp.bfloat16)
+
+    start = pl.multiple_of(late * half, half)
+    pltpu.make_async_copy(last_ref, polar_ref.at[:, pl.ds(start, half)], sems.at[late]).start()
     packed = m_ref.shape[0]
-    tile = 256
+
     for a in range(0, packed, tile):
-        round_ref[a:a + tile, a:] = m_ref[a:a + tile, a:].astype(jnp.bfloat16)
+        round_ref[a:a + tile, a:] = (m_ref[a:a + tile, a:] + lax.dot_general(
+            late_ref[a:a + tile], late_ref[a:], (((1,), (1,)), ((), ())),
+            preferred_element_type=jnp.float32)).astype(jnp.bfloat16)
 
     def apply(v):
         parts = []
@@ -547,18 +593,27 @@
 
     w = w_ref[...]
     q = lead_ref[...].astype(jnp.float32).T
-    u = apply((q * w).astype(jnp.bfloat16))
-    u += apply((u * (w * factor)).astype(jnp.bfloat16))
+    v_ref[...] = (q * w).astype(jnp.bfloat16)
+    u_ref[...] = jnp.zeros_like(u_ref)
+
+    @pl.loop(0, DYSON)
+    def _(_):
+        u = apply(v_ref[...])
+        u_ref[...] += u
+        v_ref[...] = (u * (w_ref[...] * factor)).astype(jnp.bfloat16)
+
+    u = u_ref[...]
     last = (q + factor * u).astype(jnp.bfloat16)
     screen_ref[...] = lax.dot_general(
         at_ref[...], last, (((1,), (1,)), ((), ())), preferred_element_type=jnp.float32)
-    for copy in copies:
-        copy.wait()
-
-
-def finish(low, high, at, m, w, lead):
-    count, halves, width, half = low.shape
-    units = 2 * count * halves
+    for k in range(units):
+        copy(k).wait()
+
+
+def finish(*streamed):
+    tiles, at = streamed[:4], streamed[4]
+    count, halves, width, half = tiles[0].shape
+    units = len(tiles) * count * halves
     packed = at.shape[1]
     vmem = pl.BlockSpec(memory_space=pltpu.VMEM)
     return pl.pallas_call(
@@ -567,16 +622,19 @@
             jax.ShapeDtypeStruct((width, units * half), jnp.bfloat16),
             jax.ShapeDtypeStruct((width, CW), jnp.float32),
         ),
-        in_specs=[vmem] * 6,
+        in_specs=[vmem] * 9,
         out_specs=(pl.BlockSpec(memory_space=pl.ANY), vmem),
         scratch_shapes=[
             pltpu.VMEM((packed, packed), jnp.bfloat16),
+            pltpu.VMEM((width, half), jnp.bfloat16),
+            pltpu.VMEM((CW, packed), jnp.bfloat16),
+            pltpu.VMEM((CW, packed), jnp.float32),
             pltpu.SemaphoreType.DMA((units,)),
         ],
         compiler_params=pltpu.CompilerParams(vmem_limit_bytes=FINISH_LIMIT),
     )(*(
         pltpu.with_memory_space_constraint(value, pltpu.VMEM)
-        for value in (low, high, at, m, w, lead)
+        for value in streamed
     ))
 
 

time: 105 us -> 101 us (0.962)
  Pallas kernels: 104 us -> 99.8 us
    pallas_call x1, Pallas kernels: 96.2 us -> 92 us  [stream(): pl.pallas_call(stream_kernel, out_shape=(*(pltpu.VMEM((nz // 2, 2, width,...]
where the time goes in v3:
time: 101 us
  Pallas kernels  99.8 us (99%)
    pallas_call x1, Pallas kernels, stream(): pl.pallas_call(stream_kernel, out_shape=(*(pltpu.VMEM((nz // 2, 2, width,...  92 us
    pallas_call x1, Pallas kernels, finish(): pl.pallas_call(functools.partial(finish_kernel, 8.0 / G), out_shape=(jax....  7.8 us

profile of v3, /device:TPU:0, one launch (start us, length us, event | category | flops | bytes accessed | tf_op | source)
XLA Modules:
  0.0 100.6 jit_solution(4826367918147326223)
XLA Ops:
  0.6 92.0 %shard_map.59 = (bf16[2,2,1024,512]{3,2,1,0:T(8,128)(2,1)S(1)}, bf16[2,2,1024,512]{3,2,1,0:T(8,128)(2,1)S(1)}, bf16[2,2,1024,512]{3,2,1,0:T(8,128)(2,1)S(1)}, bf...) custom-call(bf16[512,1024]{1,0:T(8,128)(2,1)} %rows_ref.1, ...), custom_call_target="tpu_custom_call" | custom-call | tf_op jit(solution)/shard_map/pallas_call | solution.py:506
  92.6 7.8 %shard_map.60 = (bf16[1024,8192]{1,0:T(8,128)(2,1)}, f32[1024,128]{1,0:T(8,128)}) custom-call(bf16[2,2,1024,512]{3,2,1,0:T(8,128)(2,1)S(1)} %get-tuple-element.13.tiles0_ref, bf16[2,2,1024,512]{3,2,1,0:T(8,128)(2,1)S(1)} %get-tuple-element.14.tiles1_ref, bf16[2,2,1024,512]{3,2,1,0:T(8,128)(2,1)S(1)} %get-tuple-element.15.tiles2_ref, ...), custom_call_target="tpu_custom_call" | custom-call | tf_op jit(solution)/shard_map/pallas_call | solution.py:619

commit v4 on v3

--- a/solution.py
+++ b/solution.py
@@ -26,31 +26,31 @@
 PLANS = (
     (
         (
-            0, 1, 68, 32, 2, 3, 16, 69, 18, 84, 19, 17, 50, 71, 34, 70, 48,
+            0, 1, 68, 2, 3, 16, 69, 48, 17, 35, 18, 19, 34, 71, 84, 70,
         ),
         (
-            2, 1, 0, 4, 5, 3, 7, 12, 13, 6, 9, 14, 11, 15, 10, 8,
+            0, 1, 2, 3, 4, 5, 12, 7, 13, 6, 9, 14, 11, 8, 15, 10,
         ),
         (
-            (), (101,), (76,), (), (85,), (51, 49), (35, 86, 87, 103), (92, 102, 33, 117, 78),
-            (), (79,), (), (135, 108, 77, 94), (), (75, 95), (), (93, 73, 116), (), (100, 118,
-            111, 91, 72), (), (89, 107), (110, 74), (124, 126), (105, 143), (109, 125, 139,
-            121), (120, 104), (), (), (122, 106, 90, 88), (), (), (), (),
+            (33,), (32,), (), (50, 78), (49,), (51, 86, 76, 101), (103, 87), (94,), (79, 77,
+            102, 85), (), (), (92, 75, 116, 135, 117, 100, 110), (), (108, 95), (), (118, 73,
+            93), (), (91, 74), (), (89, 72), (121, 126), (124, 107, 105, 111), (), (139, 90),
+            (88, 109), (), (), (125, 143, 122, 106, 120, 104), (), (), (), (),
         ),
         (),
     ),
     (
         (
-            0, 1, 68, 2, 3, 16, 17, 70, 74, 76, 72, 19, 84, 18, 78, 75, 69, 71, 73, 102,
+            0, 1, 68, 2, 3, 76, 70, 72, 17, 32, 100, 69, 33, 16, 18, 74, 19, 84, 71, 78, 77, 116,
         ),
         (
-            0, 1, 4, 6, 3, 8, 2, 12, 14, 10, 9, 13, 7, 5, 11, 15,
+            0, 4, 1, 2, 6, 8, 3, 10, 5, 13, 14, 9, 12, 7, 11, 15,
         ),
         (
-            (), (86,), (49, 100, 79, 116), (90, 118, 34), (77, 35), (33, 88), (117,), (104, 51,
-            48), (), (32,), (126, 108, 92, 50, 94), (110,), (124, 91), (), (), (121, 101, 106,
-            125, 120), (89, 107, 122, 85), (), (), (103, 87, 95), (), (93, 105), (), (135,),
-            (111, 109), (), (), (139,), (143,), (), (), (),
+            (), (79, 86, 49), (92,), (102, 75), (48,), (104, 118, 85, 73, 34, 50, 35, 121, 88),
+            (), (117, 90), (108,), (), (126, 124), (51, 101, 122), (120, 106), (87,), (), (93,),
+            (95,), (125, 110), (94, 109), (91, 103), (89,), (), (), (135,), (107, 111), (105,),
+            (), (139,), (143,), (), (), (),
         ),
         (),
     ),
@@ -303,11 +303,6 @@
         value = value * root_ref[:, pl.ds(pl.multiple_of(b * width + h * half, half), half)]
         p_ref[b, h, pl.ds(start, second if kind else first)] = value.astype(jnp.bfloat16)
 
-    for h in range(2):
-        keep_rows[h].wait()
-        rows_pair(h, 1 - c).wait_recv()
-        spare_ref[h] = dot(pick_s[...], raw(1, h)).astype(jnp.bfloat16)
-        surplus_x(h).start()
     def prepare(h):
         surplus_x(h).wait_recv()
         surplus_pair(h, c).start()
@@ -329,7 +324,7 @@
             send(ox, ob, p, s_pair.at[ox, ob, p], to_pair).wait_recv()
         return moves(t, k, p, zz, ox, ob, "start")
 
-    def moves(t, k, p, zz, ox, ob, act):
+    def moves(t, k, p, zz, ox, ob, act, across=True):
         def do(make):
             getattr(make(), act)()
 
@@ -340,7 +335,8 @@
                 do(lambda: over_in(ox, ob, p))
                 pl.when(middle)(lambda: do(lambda: over_out(ox, ob, p)))
             do(lambda: over_y(ox, ob, p))
-            do(lambda: over_x(ox, ob, p))
+            if across:
+                do(lambda: over_x(ox, ob, p))
         elif t == ZD:
             pl.when(middle)(lambda: do(lambda: onward(ox, zz, ob, p)))
         elif t == XO:
@@ -401,10 +397,17 @@
         w_ref[...] = -2.0 * energy / (energy * energy + frequency * frequency) * (
             1.0 / math.sqrt(4 * slots))
 
-    keep_root.wait()
     for h in range(2):
+        keep_rows[h].wait()
+        rows_pair(h, 1 - c).wait_recv()
+        spare_ref[h] = dot(pick_s[...], raw(1, h)).astype(jnp.bfloat16)
+        surplus_x(h).start()
+        if h == 0:
+            keep_root.wait()
         fill(0, h, dot(pick_a[:, :slots], raw(0, h)) + dot(pick_a[:, slots:], raw(1, h)))
-        event(h)
+        moves(OWN, 0, h, z, x, b, "start", across=False)
+    for h in range(2):
+        over_x(x, b, h).start()
     weights()
     run([[code for code in plan[0] if code not in (0, 1)] for plan in PLANS])
 
@@ -471,25 +474,43 @@
     slot_events(2 * units - 1)
     run([plan[3] for plan in PLANS])
     ob, h = place_of(units - 1, units, edge, z, y, nz)
-    ready(ob, h)
-    hand_on(1).start()
+
+    def hand_item(ox, cc, kind):
+        start = pl.multiple_of(ox * share + cc * core + (first if kind else 0), 64)
+        rows = pl.ds(start, second if kind else first)
+        sem = s_late.at[1 + ox * 4 + kind * 2 + jnp.where(cc == c, 0, 1)]
+        return pltpu.make_async_copy(p_ref.at[ob, h, rows], late_ref.at[rows, half:], sem)
+
+    def finish_sends(codes):
+        for code in codes:
+            t, k, p = code // 16, code // 4 % 4, code % 4
+            zz = far_plane(z, nz, k) if k else z
+            ox = x if t in (OWN, YO, ZN, YN) else 1 - x
+            ob = zz * 2 + (y if t in (OWN, XO, ZN, XN) else 1 - y)
+            moves(t, k, p, zz, ox, ob, "wait_send")
+
+    quarters = [(ox, kind) for ox in range(2) for kind in range(2)]
+    for ox, kind in quarters:
+        hand_item(ox, c, kind).start()
+    recent = {
+        code for plan in PLANS for codes in (*plan[2][2 * units - 8:], plan[3]) for code in codes}
     lead_ref[...] = p_ref[0, 0, :, :CW]
-
-    for k in range(2):
-        hand_on(k).wait()
     energy_to(0, to_x, g).wait_send()
     energy_to(1, to_pair, g).wait_send()
     energy_to(2, to_pair, g_x).wait_send()
-    for h in range(2):
-        rows_pair(h, c).wait_send()
-        surplus_x(h).wait_send()
-        surplus_pair(h, c).wait_send()
-    for code in EVENTS:
-        t, k, p = code // 16, code // 4 % 4, code % 4
-        zz = far_plane(z, nz, k) if k else z
-        ox = x if t in (OWN, YO, ZN, YN) else 1 - x
-        ob = zz * 2 + (y if t in (OWN, XO, ZN, XN) else 1 - y)
-        moves(t, k, p, zz, ox, ob, "wait_send")
+    for k in range(2):
+        rows_pair(k, c).wait_send()
+        surplus_x(k).wait_send()
+        surplus_pair(k, c).wait_send()
+    hand_on(0).wait()
+    finish_sends([code for code in EVENTS if code not in recent])
+    for ox, kind in quarters:
+        from_pair(ox, ob, kind, h)
+        hand_item(ox, 1 - c, kind).start()
+    finish_sends([code for code in EVENTS if code in recent])
+    for ox, kind in quarters:
+        hand_item(ox, c, kind).wait()
+        hand_item(ox, 1 - c, kind).wait()
 
 
 def stream(pair_density, energies, batch_live, coulomb_root, blocks):
@@ -530,7 +551,7 @@
             pltpu.VMEM((1, coulomb_root.shape[0]), f32),
             dma((2, blocks, 2, 4)), dma((blocks, 4)), dma((2, nz, 4)), dma((2, 2, nz, 4)),
             dma((2, blocks, 4)), dma((5,)), dma((2,)), dma((2,)), dma((2, 2)), dma((2, 2)),
-            dma((3,)), dma((4,)), dma((2,)),
+            dma((3,)), dma((4,)), dma((9,)),
         ],
         compiler_params=pltpu.CompilerParams(
             collective_id=0, has_side_effects=True, vmem_limit_bytes=VMEM_LIMIT),

time: 101 us -> 99.4 us (0.984)
  Pallas kernels: 99.8 us -> 98.4 us
    pallas_call x1, Pallas kernels: 92 us -> 90.6 us  [stream(): pl.pallas_call(stream_kernel, out_shape=(*(pltpu.VMEM((nz // 2, 2, width,...]
where the time goes in v4:
time: 99.4 us; the launch traced here: 99.2 us
  Pallas kernels  98.4 us (99%)
    pallas_call x1, Pallas kernels, stream(): pl.pallas_call(stream_kernel, out_shape=(*(pltpu.VMEM((nz // 2, 2, width,...  90.6 us
    pallas_call x1, Pallas kernels, finish(): pl.pallas_call(functools.partial(finish_kernel, 8.0 / G), out_shape=(jax....  7.79 us

profile of v4, /device:TPU:0, one launch (start us, length us, event | category | flops | bytes accessed | tf_op | source)
XLA Modules:
  0.0 99.2 jit_solution(13382721774521691860)
XLA Ops:
  0.6 90.6 %shard_map.59 = (bf16[2,2,1024,512]{3,2,1,0:T(8,128)(2,1)S(1)}, bf16[2,2,1024,512]{3,2,1,0:T(8,128)(2,1)S(1)}, bf16[2,2,1024,512]{3,2,1,0:T(8,128)(2,1)S(1)}, bf...) custom-call(bf16[512,1024]{1,0:T(8,128)(2,1)} %rows_ref.1, ...), custom_call_target="tpu_custom_call" | custom-call | tf_op jit(solution)/shard_map/pallas_call | solution.py:527
  91.3 7.8 %shard_map.60 = (bf16[1024,8192]{1,0:T(8,128)(2,1)}, f32[1024,128]{1,0:T(8,128)}) custom-call(bf16[2,2,1024,512]{3,2,1,0:T(8,128)(2,1)S(1)} %get-tuple-element.13.tiles0_ref, bf16[2,2,1024,512]{3,2,1,0:T(8,128)(2,1)S(1)} %get-tuple-element.14.tiles1_ref, bf16[2,2,1024,512]{3,2,1,0:T(8,128)(2,1)S(1)} %get-tuple-element.15.tiles2_ref, ...), custom_call_target="tpu_custom_call" | custom-call | tf_op jit(solution)/shard_map/pallas_call | solution.py:640

commit v5 on v4

--- a/solution.py
+++ b/solution.py
@@ -206,11 +206,13 @@
         greet(to)
     pl.when(middle)(lambda: greet(to_out))
 
-    def rows_pair(h, who):
+    def rows_pair(h, tail, who):
+        rows = pl.ds(2 * first if tail else 0, slots - 2 * first if tail else 2 * first)
+        columns = slice(h * half, (h + 1) * half)
         return pltpu.make_async_remote_copy(
-            src_ref=rows_ref.at[:, h * half:(h + 1) * half],
-            dst_ref=raw_ref.at[who, :, h * half:(h + 1) * half],
-            send_sem=s_raw.at[h], recv_sem=r_raw.at[h], device_id=to_pair, device_id_type=MESH)
+            src_ref=rows_ref.at[rows, columns], dst_ref=raw_ref.at[who, rows, columns],
+            send_sem=s_raw.at[h, tail], recv_sem=r_raw.at[h, tail], device_id=to_pair,
+            device_id_type=MESH)
 
     def energy_to(way, to, who):
         return pltpu.make_async_remote_copy(
@@ -232,7 +234,7 @@
     position = column_iota(pick_s.shape[0]) + (share + c * pick_s.shape[0])
     one_hot(pick_s, jnp.where(position < count, position - live0, -1))
     slot = column_iota(first) + c * first
-    one_hot(pick_a, jnp.where(slot < live0, slot, slots + slot - live0))
+    one_hot(pick_a, jnp.where(slot < live0, slot, 2 * first + slot - live0))
     slot = column_iota(second) + (2 * first + c * second)
     one_hot(pick_b, jnp.where(
         slot < live0, slot,
@@ -243,7 +245,8 @@
 
     g_x, g_pair, g_far = (1 - x) * 2 + c, x * 2 + 1 - c, (1 - x) * 2 + 1 - c
     for h in range(2):
-        rows_pair(h, c).start()
+        for tail in range(2):
+            rows_pair(h, tail, c).start()
     energy_to(0, to_x, g).start()
     energy_to(1, to_pair, g).start()
 
@@ -399,13 +402,16 @@
 
     for h in range(2):
         keep_rows[h].wait()
-        rows_pair(h, 1 - c).wait_recv()
+        rows_pair(h, 0, 1 - c).wait_recv()
+        if h == 0:
+            keep_root.wait()
+        head = 2 * first
+        fill(0, h, dot(pick_a[:, :head], raw_ref[0, :head, h * half:(h + 1) * half]) + dot(
+            pick_a[:, head:], raw_ref[1, :head, h * half:(h + 1) * half]))
+        moves(OWN, 0, h, z, x, b, "start", across=False)
+        rows_pair(h, 1, 1 - c).wait_recv()
         spare_ref[h] = dot(pick_s[...], raw(1, h)).astype(jnp.bfloat16)
         surplus_x(h).start()
-        if h == 0:
-            keep_root.wait()
-        fill(0, h, dot(pick_a[:, :slots], raw(0, h)) + dot(pick_a[:, slots:], raw(1, h)))
-        moves(OWN, 0, h, z, x, b, "start", across=False)
     for h in range(2):
         over_x(x, b, h).start()
     weights()
@@ -499,7 +505,8 @@
     energy_to(1, to_pair, g).wait_send()
     energy_to(2, to_pair, g_x).wait_send()
     for k in range(2):
-        rows_pair(k, c).wait_send()
+        rows_pair(k, 0, c).wait_send()
+        rows_pair(k, 1, c).wait_send()
         surplus_x(k).wait_send()
         surplus_pair(k, c).wait_send()
     hand_on(0).wait()
@@ -544,13 +551,13 @@
             pltpu.VMEM((4, 1, slots), f32),
             pltpu.VMEM((4 * slots, LANES), f32),
             pltpu.VMEM((1, packed), jnp.int32),
-            pltpu.VMEM((first, 2 * slots), bf16),
+            pltpu.VMEM((first, 4 * first), bf16),
             pltpu.VMEM((second, 2 * slots + 2 * spare), bf16),
             pltpu.VMEM((spare, slots), bf16),
             pltpu.SMEM((4,), jnp.int32),
             pltpu.VMEM((1, coulomb_root.shape[0]), f32),
             dma((2, blocks, 2, 4)), dma((blocks, 4)), dma((2, nz, 4)), dma((2, 2, nz, 4)),
-            dma((2, blocks, 4)), dma((5,)), dma((2,)), dma((2,)), dma((2, 2)), dma((2, 2)),
+            dma((2, blocks, 4)), dma((5,)), dma((2, 2)), dma((2, 2)), dma((2, 2)), dma((2, 2)),
             dma((3,)), dma((4,)), dma((9,)),
         ],
         compiler_params=pltpu.CompilerParams(

time: 99.4 us -> 99.4 us (level)
  no operation moved by 1% of the time
where the time goes in v5:
time: 99.4 us; the launch traced here: 99.3 us
  Pallas kernels  98.5 us (99%)
    pallas_call x1, Pallas kernels, stream(): pl.pallas_call(stream_kernel, out_shape=(*(pltpu.VMEM((nz // 2, 2, width,...  90.7 us
    pallas_call x1, Pallas kernels, finish(): pl.pallas_call(functools.partial(finish_kernel, 8.0 / G), out_shape=(jax....  7.79 us

profile of v5, /device:TPU:0, one launch (start us, length us, event | category | flops | bytes accessed | tf_op | source)
XLA Modules:
  0.0 99.3 jit_solution(7641659340564340432)
XLA Ops:
  0.6 90.7 %shard_map.59 = (bf16[2,2,1024,512]{3,2,1,0:T(8,128)(2,1)S(1)}, bf16[2,2,1024,512]{3,2,1,0:T(8,128)(2,1)S(1)}, bf16[2,2,1024,512]{3,2,1,0:T(8,128)(2,1)S(1)}, bf...) custom-call(bf16[512,1024]{1,0:T(8,128)(2,1)} %rows_ref.1, ...), custom_call_target="tpu_custom_call" | custom-call | tf_op jit(solution)/shard_map/pallas_call | solution.py:534
  91.3 7.8 %shard_map.60 = (bf16[1024,8192]{1,0:T(8,128)(2,1)}, f32[1024,128]{1,0:T(8,128)}) custom-call(bf16[2,2,1024,512]{3,2,1,0:T(8,128)(2,1)S(1)} %get-tuple-element.13.tiles0_ref, bf16[2,2,1024,512]{3,2,1,0:T(8,128)(2,1)S(1)} %get-tuple-element.14.tiles1_ref, bf16[2,2,1024,512]{3,2,1,0:T(8,128)(2,1)S(1)} %get-tuple-element.15.tiles2_ref, ...), custom_call_target="tpu_custom_call" | custom-call | tf_op jit(solution)/shard_map/pallas_call | solution.py:647
